TPU v7x, 32 devices: a whole 2x2x4 slice. The times are simulated.
32 devices in a mesh: roll: 4 (over y, x), seq: 8 (over z, core).
Axes of the slice: x: 2, y: 2, z: 4, core: 2. Of those that a mesh axis runs over, the one named last changes fastest.
Arguments:
- query_rows: bfloat16 [4, 4096, 1792], P('roll', 'seq'), may hold values from -200 to 200
- key_rows: bfloat16 [4, 4096, 256], P('roll', 'seq'), may hold values from -6 to 6
- value_rows: bfloat16 [4, 4096, 256], P('roll', 'seq'), may hold values from -6 to 6
- cotangent: bfloat16 [4, 4096, 1792], P('roll', None, 'seq'), may hold values from -6 to 6
- slopes: float32 [14], replicated, may hold values from 0.00029296876 to 0.0390625
- lengths: int32 [4], P('roll'), may hold values from 1024 to 4096, as said below
- loss_mask: int32 [4, 4096], P('roll', 'seq'), may hold values 0 or 1
- distances: int32 [4], P('roll'), may hold values from 40 to 357
Outputs:
- grad_queries: bfloat16 [4, 4096, 1792], P('roll', 'seq')
- grad_keys: bfloat16 [4, 4096, 256], P('roll', 'seq')
- grad_values: bfloat16 [4, 4096, 256], P('roll', 'seq')
Inputs may be any that keep to these rules, and one draw needn't show every extreme that they name: `lengths`: some rollout has 4096 tokens and some 4096 // 4.
All inputs are finite; a program needn't handle non-finite values. No bound on the sum of `loss_mask` on one device may be relied on, other than what follows from the above.
Results may differ from a plain program's by a relative error of at most 0.0068.
Values may be sent and summed in bfloat16 or wider, within the bound.
No kernel may reach another device: no remote copies, remote signals or barrier semaphores. Data moves between devices by JAX's collectives and lax.ppermute only.
A program may use at most 64 MiB of HBM per device.

v0:
```python
import math

import jax
import jax.numpy as jnp
from jax import lax
from jax.sharding import PartitionSpec as P

HEAD_DIM = 128
WINDOW = 1024


def passed_along(value, axis, steps):
    count = lax.axis_size(axis)
    leading, last = (max(0, -steps), min(count, count - steps))
    return lax.ppermute(value, axis, [(source, source + steps) for source in range(leading, last)])


def shards(query_rows, key_rows, value_rows, cotangent, slopes, lengths, loss_mask, distances):
    own_q = query_rows[0]
    own_k = key_rows[0]
    own_v = value_rows[0]
    tok_rows = own_q.shape[0]
    features = own_q.shape[1]
    kv_features = own_k.shape[1]
    head_dim = HEAD_DIM
    head_count = features // head_dim
    kv_count = kv_features // head_dim
    group_size = head_count // kv_count
    band_reach = (WINDOW - 2) // tok_rows + 1
    band_len = (band_reach + 1) * tok_rows
    seq_len = tok_rows * lax.axis_size("seq")
    seq_pos = lax.axis_index("seq")
    attn_scale = 1.0 / math.sqrt(head_dim)
    positions = seq_pos * tok_rows + jnp.arange(tok_rows, dtype=jnp.int32)
    valid = ((positions < lengths[0]) & (loss_mask[0] == 1)).astype(jnp.float32)
    local_count = jnp.sum(valid)
    my_distance = distances[0].astype(jnp.float32)
    count_all = lax.psum(local_count, "seq")
    group_total = lax.psum(my_distance, "roll")
    advantage = (group_total / lax.axis_size("roll") - my_distance) / 64.0
    weight = advantage * valid * seq_len / (1.0 + count_all)
    arrived = lax.all_to_all(cotangent, "seq", split_axis=1, concat_axis=2, tiled=True)[0]
    dout = (arrived.astype(jnp.float32) * weight[:, None]).astype(jnp.bfloat16)
    kv_pair = jnp.stack([own_k, own_v])
    earlier = []
    for offset in range(1, band_reach + 1):
        earlier.append(passed_along(kv_pair, "seq", offset))
    ordered = earlier[::-1]
    band_k = jnp.concatenate([blk[0] for blk in ordered] + [own_k], 0)
    band_v = jnp.concatenate([blk[1] for blk in ordered] + [own_v], 0)
    key_pos = (seq_pos - band_reach) * tok_rows + jnp.arange(band_len, dtype=jnp.int32)
    pos_gap = positions[:, None] - key_pos[None, :]
    allowed = (pos_gap >= 0) & (pos_gap < WINDOW) & (key_pos[None, :] >= 0)
    gap_float = pos_gap.astype(jnp.float32)
    split_at = band_reach * tok_rows
    contract_rows = (((0,), (0,)), ((), ()))

    def head_step(head, carry):
        grad_q, own_dk, own_dv, part_k, part_v = carry
        column = head * head_dim
        kv_column = head // group_size * head_dim
        q_head = lax.dynamic_slice_in_dim(own_q, column, head_dim, 1)
        k_head = lax.dynamic_slice_in_dim(band_k, kv_column, head_dim, 1)
        v_head = lax.dynamic_slice_in_dim(band_v, kv_column, head_dim, 1)
        d_head = lax.dynamic_slice_in_dim(dout, column, head_dim, 1)
        slope = lax.dynamic_index_in_dim(slopes, head, keepdims=False)
        scores = (
            jnp.dot(q_head, k_head.T, preferred_element_type=jnp.float32) * attn_scale
            - slope * gap_float
        )
        masked = jnp.where(allowed, scores, -jnp.inf)
        row_max = jnp.max(masked, axis=1, keepdims=True)
        exp_terms = jnp.where(allowed, jnp.exp(masked - row_max), 0.0)
        probs = exp_terms / jnp.sum(exp_terms, axis=1, keepdims=True)
        probs_low = probs.astype(jnp.bfloat16)
        dprob = jnp.dot(d_head, v_head.T, preferred_element_type=jnp.float32)
        row_delta = jnp.sum(probs * dprob, axis=1, keepdims=True)
        dscore = (probs * (dprob - row_delta) * attn_scale).astype(jnp.bfloat16)
        head_dq = jnp.dot(dscore, k_head, preferred_element_type=jnp.float32).astype(jnp.bfloat16)
        band_dk = lax.dot_general(dscore, q_head, contract_rows, preferred_element_type=jnp.float32)
        band_dv = lax.dot_general(
            probs_low, d_head, contract_rows, preferred_element_type=jnp.float32
        )
        grad_q = lax.dynamic_update_slice_in_dim(grad_q, head_dq, column, 1)
        own_dk = lax.dynamic_update_slice_in_dim(
            own_dk,
            lax.dynamic_slice_in_dim(own_dk, kv_column, head_dim, 1) + band_dk[split_at:],
            kv_column,
            1,
        )
        own_dv = lax.dynamic_update_slice_in_dim(
            own_dv,
            lax.dynamic_slice_in_dim(own_dv, kv_column, head_dim, 1) + band_dv[split_at:],
            kv_column,
            1,
        )
        far_dk = band_dk[:split_at].reshape(band_reach, tok_rows, head_dim)
        far_dv = band_dv[:split_at].reshape(band_reach, tok_rows, head_dim)
        part_k = lax.dynamic_update_slice_in_dim(
            part_k, lax.dynamic_slice_in_dim(part_k, kv_column, head_dim, 2) + far_dk, kv_column, 2
        )
        part_v = lax.dynamic_update_slice_in_dim(
            part_v, lax.dynamic_slice_in_dim(part_v, kv_column, head_dim, 2) + far_dv, kv_column, 2
        )
        return (grad_q, own_dk, own_dv, part_k, part_v)

    start_carry = (
        jnp.zeros((tok_rows, features), jnp.bfloat16),
        jnp.zeros((tok_rows, kv_features), jnp.float32),
        jnp.zeros((tok_rows, kv_features), jnp.float32),
        jnp.zeros((band_reach, tok_rows, kv_features), jnp.float32),
        jnp.zeros((band_reach, tok_rows, kv_features), jnp.float32),
    )
    grad_q, total_k, total_v, part_k, part_v = lax.fori_loop(0, head_count, head_step, start_carry)
    part_k = part_k.astype(jnp.bfloat16)
    part_v = part_v.astype(jnp.bfloat16)
    for offset in range(1, band_reach + 1):
        outgoing = jnp.stack([part_k[band_reach - offset], part_v[band_reach - offset]])
        incoming = passed_along(outgoing, "seq", -offset)
        total_k = total_k + incoming[0].astype(jnp.float32)
        total_v = total_v + incoming[1].astype(jnp.float32)
    return (grad_q[None], total_k.astype(jnp.bfloat16)[None], total_v.astype(jnp.bfloat16)[None])


def solution(mesh):
    placed = (
        P("roll", "seq", None),
        P("roll", "seq", None),
        P("roll", "seq", None),
        P("roll", None, "seq"),
        P(),
        P("roll"),
        P("roll", "seq"),
        P("roll"),
    )
    return jax.shard_map(
        shards,
        mesh=mesh,
        in_specs=placed,
        out_specs=(P("roll", "seq", None), P("roll", "seq", None), P("roll", "seq", None)),
        check_vma=False,
    )
```

profile of v0, /device:TPU:1, one launch (start us, length us, event | category | flops | bytes accessed | tf_op | source)
XLA Modules:
  0.0 346.7 jit_solution(13123298232539514425)
XLA Ops:
  0.6 10.0 %copy.19 = bf16[1,4096,224]{2,0,1:T(2,128)(2,1)} copy(bf16[1,4096,224]{1,2,0:T(8,128)(2,1)} %param.13) | data formatting | bytes 3670016 | tf_op args[3]
  11.1 23.6 %reduce.2 = bf16[4096,224]{1,0:T(8,128)(2,1)S(1)} reduce(bf16[4096,1,224]{2,1,0:T(2,128)(2,1)} %bitcast.71, bf16[]{:T(256)} %broadcast.76), dimensions={1}, to_apply=%bitcast.53.reduce_sub_computation | reduce | bytes 3670018
  34.8 5.2 %reshape.80 = bf16[8,2,57344]{2,1,0:T(2,128)(2,1)} reshape(bf16[4096,224]{1,0:T(8,128)(2,1)S(1)} %reduce.2) | data formatting | bytes 3670016
  40.0 6.5 %all-to-all-start = ((bf16[8,2,57344]{2,1,0:T(2,128)(2,1)}), bf16[8,2,57344]{2,1,0:T(2,128)(2,1)S(1)}, u32[]{:S(2)}, u32[]{:S(2)}) async-start(bf16[8,2,57344]{2,1,0:T(2,128)(2,1)} %reshape.80), calls=%async_computation | async-start | bytes 3670016 | tf_op jit(solution)/shard_map/all_to_all | solution.py:42
  47.9 3.5 %collective-permute-start.1 = (bf16[2,512,256]{2,1,0:T(8,128)(2,1)}, bf16[2,512,256]{2,1,0:T(8,128)(2,1)}, u32[]{:S(2)}, u32[]{:S(2)}) collective-permute-start(bf16[2,512,256]{2,1,0:T(8,128)(2,1)} %constant_dynamic-update-slice_fusion), channel_id=1, source_target_pairs={{0,1},{1,2},{2,3},{3,4},{4,5},{5,6},{6,7},{8,9},{9,10},{10,11},{11... | collective-permute-start | bytes 1572872 | tf_op jit(solution)/shard_map/ppermute | solution.py:15
  56.5 9.1 %psum.14 = f32[]{:T(128)} all-reduce(f32[]{:T(128)} %bitcast.7), channel_id=1, replica_groups=mesh['roll'=4,'seq'=8] {'roll'}, use_global_device_ids=true, to_apply=%region_0.0 | all-reduce | flops 1 | bytes 8 | tf_op jit(solution)/shard_map/psum | solution.py:39
  65.7 36.1 %psum.15 = f32[]{:T(128)} all-reduce(f32[]{:T(128)} %convert_reduce_fusion), channel_id=1, replica_groups=mesh['roll'=4,'seq'=8] {'seq'}, use_global_device_ids=true, to_apply=%region_2.0 | all-reduce | flops 1 | bytes 8 | tf_op jit(solution)/shard_map/psum | solution.py:38
  105.5 5.8 %reshape.81 = bf16[4096,1,224]{2,1,0:T(2,128)(2,1)} reshape(bf16[8,2,57344]{2,1,0:T(2,128)(2,1)S(1)} %all-to-all-done) | data formatting | bytes 3670016
  111.3 10.1 %copy.20 = bf16[1,4096,224]{1,2,0:T(8,128)(2,1)S(1)} copy(bf16[1,4096,224]{2,0,1:T(2,128)(2,1)} %bitcast.72) | data formatting | bytes 3670016 | tf_op jit(solution)/shard_map/all_to_all | solution.py:42
  130.6 186.0 %while.25 = (s32[]{:T(128)}, bf16[512,1792]{1,0:T(8,128)(2,1)}, f32[512,256]{1,0:T(8,128)S(1)}, f32[512,256]{1,0:T(8,128)S(1)}, f32[2,512,256]{2,1,0:T(8,128)S(1...) while((s32[]{:T(128)}, bf16[512,1792]{1,0:T(8,128)(2,1)}, ...), condition=%wide.region_7.8_spmd.clone.clone, body=%wide.region_3.7_spmd.clone.clone.sunk | while | flops 1033828864 | bytes 46446556 | solution.py:114
  131.2 3.3 fusion.59
  144.4 3.3 fusion.59
  157.7 3.3 fusion.59
  171.0 3.3 fusion.59
  184.2 3.3 fusion.59
  197.5 3.3 fusion.59
  237.3 3.3 fusion.59
  250.7 3.3 fusion.59
  264.0 3.3 fusion.59
  277.3 3.3 fusion.59
  290.6 3.3 fusion.59
  303.9 3.3 fusion.59
  320.4 19.8 %collective-permute-done.3 = bf16[2,512,256]{2,1,0:T(8,128)(2,1)S(1)} collective-permute-done((bf16[2,512,256]{2,1,0:T(8,128)(2,1)S(1)}, bf16[2,512,256]{2,1,0:T(8,128)(2,1)S(1)}, u32[]{:S(2)}, u32[]{:S(2)}) %collective-permute-start.3) | collective-permute-done | bytes 524320 | tf_op jit(solution)/shard_map/ppermute | solution.py:15
  340.2 5.6 %collective-permute-done.2 = bf16[2,512,256]{2,1,0:T(8,128)(2,1)S(1)} collective-permute-done((bf16[2,512,256]{2,1,0:T(8,128)(2,1)S(1)}, bf16[2,512,256]{2,1,0:T(8,128)(2,1)S(1)}, u32[]{:S(2)}, u32[]{:S(2)}) %collective-permute-start.2) | collective-permute-done | bytes 524320 | tf_op jit(solution)/shard_map/ppermute | solution.py:15
  (254 shorter events, 167.0 us)
Async XLA Ops:
  34.7 11.7 %copy-start.1 = (bf16[1,512,256]{2,1,0:T(8,128)(2,1)S(1)}, bf16[1,512,256]{2,1,0:T(8,128)(2,1)}, u32[]{:S(2)}) copy-start(bf16[1,512,256]{2,1,0:T(8,128)(2,1)} %param.11) | copy-start | bytes 786436
  34.8 12.4 %copy-start.2 = (bf16[1,512,256]{2,1,0:T(8,128)(2,1)S(1)}, bf16[1,512,256]{2,1,0:T(8,128)(2,1)}, u32[]{:S(2)}) copy-start(bf16[1,512,256]{2,1,0:T(8,128)(2,1)} %param.12) | copy-start | bytes 786436
  40.0 15.9 %copy-start.4 = (s32[1,512]{1,0:T(1,128)S(1)}, s32[1,512]{1,0:T(1,128)}, u32[]{:S(2)}) copy-start(s32[1,512]{1,0:T(1,128)} %param.16) | copy-start | bytes 6148
  40.0 65.5 %all-to-all-start = ((bf16[8,2,57344]{2,1,0:T(2,128)(2,1)}), bf16[8,2,57344]{2,1,0:T(2,128)(2,1)S(1)}, u32[]{:S(2)}, u32[]{:S(2)}) async-start(bf16[8,2,57344]{2,1,0:T(2,128)(2,1)} %reshape.80), calls=%async_computation | async-start | bytes 3670016 | tf_op jit(solution)/shard_map/all_to_all | solution.py:42
  47.9 55.1 %collective-permute-start.1 = (bf16[2,512,256]{2,1,0:T(8,128)(2,1)}, bf16[2,512,256]{2,1,0:T(8,128)(2,1)}, u32[]{:S(2)}, u32[]{:S(2)}) collective-permute-start(bf16[2,512,256]{2,1,0:T(8,128)(2,1)} %constant_dynamic-update-slice_fusion), channel_id=1, source_target_pairs={{0,1},{1,2},{2,3},{3,4},{4,5},{5,6},{6,7},{8,9},{9,10},{10,11},{11... | collective-permute-start | bytes 1572872 | tf_op jit(solution)/shard_map/ppermute | solution.py:15
  51.5 52.7 %collective-permute-start = (bf16[2,512,256]{2,1,0:T(8,128)(2,1)}, bf16[2,512,256]{2,1,0:T(8,128)(2,1)S(1)}, u32[]{:S(2)}, u32[]{:S(2)}) collective-permute-start(bf16[2,512,256]{2,1,0:T(8,128)(2,1)} %constant_dynamic-update-slice_fusion), channel_id=1, source_target_pairs={{0,2},{1,3},{2,4},{3,5},{4,6},{5,7},{8,10},{9,11},{10,12},{11,13},... | collective-permute-start | bytes 1572872 | tf_op jit(solution)/shard_map/ppermute | solution.py:15
  129.0 1.6 copy-start.5
  134.4 1.4 copy-start.3
  139.0 3.2 copy-start
  152.3 3.2 copy-start
  165.6 3.2 copy-start
  178.8 3.2 copy-start
  192.1 3.2 copy-start
  205.4 3.2 copy-start
  218.6 3.2 copy-start
  231.9 3.2 copy-start
  245.2 3.2 copy-start
  258.5 3.2 copy-start
  271.8 3.2 copy-start
  285.2 3.2 copy-start
  298.5 3.2 copy-start
  311.8 3.2 copy-start
  316.9 23.2 %collective-permute-start.3 = (bf16[2,512,256]{2,1,0:T(8,128)(2,1)S(1)}, bf16[2,512,256]{2,1,0:T(8,128)(2,1)S(1)}, u32[]{:S(2)}, u32[]{:S(2)}) collective-permute-start(bf16[2,512,256]{2,1,0:T(8,128)(2,1)S(1)} %pad_maximum_fusion.3), channel_id=1, source_target_pairs={{2,0},{3,1},{4,2},{5,3},{6,4},{7,5},{10,8},{11,9},{12,10},{13,11},... | collective-permute-start | bytes 1572872 | tf_op jit(solution)/shard_map/ppermute | solution.py:15
  318.3 27.5 %collective-permute-start.2 = (bf16[2,512,256]{2,1,0:T(8,128)(2,1)S(1)}, bf16[2,512,256]{2,1,0:T(8,128)(2,1)S(1)}, u32[]{:S(2)}, u32[]{:S(2)}) collective-permute-start(bf16[2,512,256]{2,1,0:T(8,128)(2,1)S(1)} %pad_maximum_fusion.2), channel_id=1, source_target_pairs={{1,0},{2,1},{3,2},{4,3},{5,4},{6,5},{7,6},{9,8},{10,9},{11,10},{12... | collective-permute-start | bytes 1572872 | tf_op jit(solution)/shard_map/ppermute | solution.py:15
  (13 other events, 17.9 us)
where the time goes:
time: 349 us; the launch traced here: 347 us
  matrix products  146 us (42%)
  other arithmetic  58.4 us (17%)
  local copies, waits for them, and re-layouts  50.5 us (14%)
  blocking collectives  45.3 us (13%)
  waiting for transfers between devices  25.4 us (7%)
  starting transfers between devices  16.5 us (5%)
    dot_general x14, matrix products, head_step(): jnp.dot(q_head, k_head.T, preferred_element_type=jnp.float32) * attn_scale  45.8 us
    dot_general x14, matrix products, head_step(): dprob = jnp.dot(d_head, v_head.T, preferred_element_type=jnp.float32)  38.8 us
    psum x1, blocking collectives, shards(): count_all = lax.psum(local_count, 'seq')  36.1 us
    unnamed x14, local copies, waits for them, and re-layouts  25.4 us
    ppermute x4, waiting for transfers between devices, passed_along(): lax.ppermute(value, axis, [(source, source + steps) for source in range(l...  25.4 us
    unnamed x1, other arithmetic  23.6 us
    dot_general x14, matrix products, head_step(): lax.dot_general(probs_low, d_head, contract_rows, preferred_element_type=...  22.3 us
    dot_general x14, matrix products, head_step(): lax.dot_general(dscore, q_head, contract_rows, preferred_element_type=jnp...  21.3 us
  transfers between devices with their start and end apart: 5, of which 2 were waited for; matrix products, arithmetic and copies ran while one was open for 1% of the time, Pallas kernels for 0%

commit v1 on v0

v1 whole, which is shorter than its diff:
```python
import functools
import math

import jax
import jax.numpy as jnp
from jax import lax
from jax.experimental import pallas as pl
from jax.experimental.pallas import tpu as pltpu
from jax.sharding import PartitionSpec as P

HEAD_DIM = 128
WINDOW = 1024
TILE = 128
FAR = -1e30
LOG2E = math.log2(math.e)


def passed_along(value, axis, steps):
    count = lax.axis_size(axis)
    leading, last = (max(0, -steps), min(count, count - steps))
    return lax.ppermute(value, axis, [(source, source + steps) for source in range(leading, last)])


def flip_kernel(x_ref, out_ref):
    out_ref[...] = x_ref[...].astype(jnp.float32).T.astype(out_ref.dtype)


def flip_blocks(x, rows):
    total, width = x.shape
    count = total // rows
    return pl.pallas_call(
        flip_kernel,
        grid=(count,),
        in_specs=[pl.BlockSpec((rows, width), lambda i: (i, 0))],
        out_specs=pl.BlockSpec((None, width, rows), lambda i: (i, 0, 0)),
        out_shape=jax.ShapeDtypeStruct((count, width, rows), x.dtype),
        name="flip_blocks",
    )(x)


def prob_kernel(group, key_tiles, invalid_ref, slope_ref, qt_ref, k_refs, v_refs, e_ref, o_ref,
                kband, vtband, bias, scores):
    kv_head = pl.program_id(0)
    sub = pl.program_id(1)
    lanes = group * TILE
    blk_rows = k_refs[0].shape[0]
    slope_row = jnp.concatenate(
        [jnp.full((1, TILE), slope_ref[kv_head * group + h] * LOG2E, jnp.float32) for h in range(group)], 1)

    @pl.when(sub == 0)
    def _():
        for n, (k_ref, v_ref) in enumerate(zip(k_refs, v_refs)):
            kband[n * blk_rows:(n + 1) * blk_rows] = k_ref[...]
            vtband[:HEAD_DIM, n * blk_rows:(n + 1) * blk_rows] = (
                v_ref[...].astype(jnp.float32).T.astype(vtband.dtype))
        vtband[HEAD_DIM:] = jnp.ones(vtband[HEAD_DIM:].shape, vtband.dtype)
        bias[...] = lax.broadcasted_iota(jnp.int32, (TILE, lanes), 0).astype(jnp.float32) * slope_row

    scale = LOG2E / math.sqrt(HEAD_DIM)
    qt = jnp.concatenate([qt_ref[h * HEAD_DIM:(h + 1) * HEAD_DIM] for h in range(group)], 1)
    below = (lax.broadcasted_iota(jnp.int32, (TILE, lanes), 0)
             > lax.broadcasted_iota(jnp.int32, (TILE, lanes), 1) % TILE)
    invalid = invalid_ref[0]
    start = pl.multiple_of(sub * TILE, TILE)
    peak = None
    shifts = []
    for t in range(key_tiles):
        k_tile = kband[pl.ds(start + t * TILE, TILE)]
        s = jnp.dot(k_tile, qt, preferred_element_type=jnp.float32) * scale + bias[...]
        if t == 0:
            s = jnp.where(below, s, FAR)
        elif t == key_tiles - 1:
            s = jnp.where(below, FAR, s)
        scores[t * TILE:(t + 1) * TILE] = s
        shift = slope_row * (t * TILE) + jnp.where(sub + t < invalid, FAR, 0.0)
        shifts.append(shift)
        top = jnp.max(s.reshape(TILE // 8, 8, lanes), 0) + shift
        peak = top if peak is None else jnp.maximum(peak, top)
    peak = jnp.max(peak, 0, keepdims=True)
    for t in range(key_tiles):
        e = jnp.exp2(scores[t * TILE:(t + 1) * TILE] - (peak - shifts[t]))
        e_ref[t * TILE:(t + 1) * TILE] = e.astype(e_ref.dtype)
    o_ref[...] = jnp.dot(vtband[:, pl.ds(start, key_tiles * TILE)], e_ref[...],
                         preferred_element_type=jnp.float32)


def grad_kernel(group, key_tiles, scale_ref, keep_ref, dt_ref, qt_ref, k_refs, v_refs, e_ref, o_ref,
                dq_ref, dk_far, dv_far, dk_own, dv_own, kband, ktband, vband, dk_acc, dv_acc, ds_all):
    sub = pl.program_id(1)
    blk_rows = k_refs[0].shape[0]
    lanes = group * TILE

    @pl.when(sub == 0)
    def _():
        for n, (k_ref, v_ref) in enumerate(zip(k_refs, v_refs)):
            rows = slice(n * blk_rows, (n + 1) * blk_rows)
            ktband[:, rows] = k_ref[...].astype(jnp.float32).T.astype(ktband.dtype)
            vband[rows] = v_ref[...]
        dk_acc[...] = jnp.zeros(dk_acc.shape, dk_acc.dtype)
        dv_acc[...] = jnp.zeros(dv_acc.shape, dv_acc.dtype)

    start = pl.multiple_of(sub * TILE, TILE)
    keep = jnp.concatenate([keep_ref[...]] * group, 1)
    inv = 1.0 / o_ref[HEAD_DIM:HEAD_DIM + 1]
    dt = jnp.concatenate([dt_ref[h * HEAD_DIM:(h + 1) * HEAD_DIM] for h in range(group)], 1)
    dt = (dt.astype(jnp.float32) * (keep * inv)).astype(jnp.bfloat16)
    qt = jnp.concatenate([qt_ref[h * HEAD_DIM:(h + 1) * HEAD_DIM] for h in range(group)], 1)
    delta = jnp.sum(dt.astype(jnp.float32) * o_ref[:HEAD_DIM], 0, keepdims=True) * inv
    over_lanes = (((1,), (1,)), ((), ()))
    for t in range(key_tiles):
        rows = pl.ds(start + t * TILE, TILE)
        e = e_ref[t * TILE:(t + 1) * TILE]
        dp = jnp.dot(vband[rows], dt, preferred_element_type=jnp.float32)
        ds = (e.astype(jnp.float32) * (dp - delta)).astype(jnp.bfloat16)
        ds_all[t * TILE:(t + 1) * TILE] = ds
        dv_acc[rows] += lax.dot_general(e, dt, over_lanes, preferred_element_type=jnp.float32)
        dk_acc[rows] += lax.dot_general(ds, qt, over_lanes, preferred_element_type=jnp.float32)
    dqt = jnp.dot(ktband[:, pl.ds(start, key_tiles * TILE)], ds_all[...],
                  preferred_element_type=jnp.float32) * scale_ref[0]
    for h in range(group):
        dq_ref[:, h * HEAD_DIM:(h + 1) * HEAD_DIM] = dqt[:, h * TILE:(h + 1) * TILE].T.astype(dq_ref.dtype)

    @pl.when(sub == pl.num_programs(1) - 1)
    def _():
        far_rows = dk_far.shape[0]
        dk_far[...] = dk_acc[:far_rows].astype(dk_far.dtype)
        dv_far[...] = dv_acc[:far_rows].astype(dv_far.dtype)
        dk_own[...] = dk_acc[far_rows:]
        dv_own[...] = dv_acc[far_rows:]


def shards(query_rows, key_rows, value_rows, cotangent, slopes, lengths, loss_mask, distances):
    own_q = query_rows[0]
    own_k = key_rows[0]
    own_v = value_rows[0]
    tok_rows, features = own_q.shape
    kv_features = own_k.shape[1]
    head_count = features // HEAD_DIM
    kv_count = kv_features // HEAD_DIM
    group = head_count // kv_count
    reach = (WINDOW - 2) // tok_rows + 1
    band_len = (reach + 1) * tok_rows
    subs = tok_rows // TILE
    key_tiles = WINDOW // TILE + 1
    keys = key_tiles * TILE
    lanes = group * TILE
    n_seq = lax.axis_size("seq")
    n_roll = lax.axis_size("roll")
    seq_len = tok_rows * n_seq
    seq_pos = lax.axis_index("seq")
    roll_pos = lax.axis_index("roll")

    kv_pair = jnp.concatenate([own_k, own_v], 1)
    bands = [passed_along(kv_pair, "seq", offset) for offset in range(reach, 0, -1)] + [kv_pair]
    flipped = flip_blocks(cotangent[0], tok_rows)
    arrived = lax.all_to_all(flipped, "seq", split_axis=0, concat_axis=0, tiled=True)
    dout_t = arrived.reshape(features, tok_rows)
    q_t = flip_blocks(own_q, tok_rows)[0]

    positions = seq_pos * tok_rows + jnp.arange(tok_rows, dtype=jnp.int32)
    valid = ((positions < lengths[0]) & (loss_mask[0] == 1)).astype(jnp.float32)
    mine = jnp.arange(n_roll) == roll_pos
    my_distance = distances[0].astype(jnp.float32)
    sums = lax.psum(
        jnp.stack([jnp.where(mine, jnp.sum(valid), 0.0), jnp.where(mine & (seq_pos == 0), my_distance, 0.0)]),
        ("roll", "seq"))
    count_all = jnp.sum(jnp.where(mine, sums[0], 0.0))
    advantage = (jnp.sum(sums[1]) / n_roll - my_distance) / 64.0
    weight = advantage * seq_len / (1.0 + count_all)

    invalid = jnp.maximum(reach - seq_pos, 0) * subs
    smem = pl.BlockSpec(memory_space=pltpu.SMEM)
    k_specs = [pl.BlockSpec((tok_rows, HEAD_DIM), lambda g, c: (0, g))] * (reach + 1)
    v_specs = [pl.BlockSpec((tok_rows, HEAD_DIM), lambda g, c: (0, kv_count + g))] * (reach + 1)
    t_spec = pl.BlockSpec((group * HEAD_DIM, TILE), lambda g, c: (g, c))
    o_rows = HEAD_DIM + 16
    e_spec = pl.BlockSpec((None, None, keys, lanes), lambda g, c: (g, c, 0, 0))
    o_spec = pl.BlockSpec((None, None, o_rows, lanes), lambda g, c: (g, c, 0, 0))
    params = pltpu.CompilerParams(vmem_limit_bytes=48 << 20)
    pairs = kv_count * group * tok_rows * keys
    e_all, o_all = pl.pallas_call(
        functools.partial(prob_kernel, group, key_tiles),
        grid=(kv_count, subs),
        in_specs=[smem, smem, t_spec, k_specs, v_specs],
        out_specs=(e_spec, o_spec),
        out_shape=(jax.ShapeDtypeStruct((kv_count, subs, keys, lanes), jnp.bfloat16),
                   jax.ShapeDtypeStruct((kv_count, subs, o_rows, lanes), jnp.float32)),
        scratch_shapes=[
            pltpu.VMEM((band_len, HEAD_DIM), jnp.bfloat16),
            pltpu.VMEM((o_rows, band_len), jnp.bfloat16),
            pltpu.VMEM((TILE, lanes), jnp.float32),
            pltpu.VMEM((keys, lanes), jnp.float32),
        ],
        compiler_params=params,
        cost_estimate=pl.CostEstimate(flops=4 * pairs * HEAD_DIM, transcendentals=pairs, bytes_accessed=2 * pairs),
        name="probs",
    )(invalid[None].astype(jnp.int32), slopes, q_t, bands, bands)

    root = 1.0 / math.sqrt(HEAD_DIM)
    far_rows = reach * tok_rows
    far = jax.ShapeDtypeStruct((far_rows, kv_features), jnp.bfloat16)
    own = jax.ShapeDtypeStruct((tok_rows, kv_features), jnp.float32)
    far_spec = pl.BlockSpec((far_rows, HEAD_DIM), lambda g, c: (0, g))
    own_spec = pl.BlockSpec((tok_rows, HEAD_DIM), lambda g, c: (0, g))
    grad_q, far_k, far_v, total_k, total_v = pl.pallas_call(
        functools.partial(grad_kernel, group, key_tiles),
        grid=(kv_count, subs),
        in_specs=[smem, pl.BlockSpec((1, TILE), lambda g, c: (0, c)), t_spec, t_spec, k_specs, v_specs,
                  e_spec, o_spec],
        out_specs=(pl.BlockSpec((TILE, lanes), lambda g, c: (c, g)), far_spec, far_spec, own_spec, own_spec),
        out_shape=(jax.ShapeDtypeStruct((tok_rows, features), jnp.bfloat16), far, far, own, own),
        scratch_shapes=[
            pltpu.VMEM((8, TILE), jnp.bfloat16),
            pltpu.VMEM((HEAD_DIM, band_len), jnp.bfloat16),
            pltpu.VMEM((band_len, HEAD_DIM), jnp.bfloat16),
            pltpu.VMEM((band_len, HEAD_DIM), jnp.float32),
            pltpu.VMEM((band_len, HEAD_DIM), jnp.float32),
            pltpu.VMEM((keys, lanes), jnp.bfloat16),
        ],
        compiler_params=params,
        cost_estimate=pl.CostEstimate(flops=8 * pairs * HEAD_DIM, transcendentals=0, bytes_accessed=2 * pairs),
        name="grads",
    )((weight * root)[None], valid[None], dout_t, q_t, bands, bands, e_all, o_all)

    for offset in range(1, reach + 1):
        rows = slice((reach - offset) * tok_rows, (reach - offset + 1) * tok_rows)
        incoming = passed_along(jnp.concatenate([far_k[rows], far_v[rows]], 1), "seq", -offset).astype(jnp.float32)
        total_k = total_k + incoming[:, :kv_features]
        total_v = total_v + incoming[:, kv_features:]
    total_k = total_k * (weight * root)
    total_v = total_v * weight
    return (grad_q[None], total_k.astype(jnp.bfloat16)[None], total_v.astype(jnp.bfloat16)[None])


def solution(mesh):
    placed = (
        P("roll", "seq", None),
        P("roll", "seq", None),
        P("roll", "seq", None),
        P("roll", None, "seq"),
        P(),
        P("roll"),
        P("roll", "seq"),
        P("roll"),
    )
    return jax.shard_map(
        shards,
        mesh=mesh,
        in_specs=placed,
        out_specs=(P("roll", "seq", None), P("roll", "seq", None), P("roll", "seq", None)),
        check_vma=False,
    )
```

time: 349 us -> 165 us (0.47)
  matrix products: 146 us -> 0 us
  other arithmetic: 58.4 us -> 3.85 us
  Pallas kernels: 0 us -> 52.3 us
  local copies, waits for them, and re-layouts: 50.5 us -> 5.55 us
  blocking collectives: 45.3 us -> 65.5 us
  waiting for transfers between devices: 25.4 us -> 17.5 us
    dot_general x70 -> x0, matrix products: 146 us -> none  [the longest x14 45.8 us: head_step(): jnp.dot(q_head, k_head.T, preferred_element_type=jnp.float32) * attn_scale]
    pallas_call x0 -> x4, Pallas kernels: none -> 52.3 us  [the longest x1 25.1 us: shards(): pl.pallas_call(functools.partial(grad_kernel, group, key_tiles), grid=(kv...]
    unnamed x1 -> x0, other arithmetic: 23.6 us -> none
    psum x2 -> x1, blocking collectives: 45.3 us -> 65.5 us  [shards(): lax.psum(jnp.stack([jnp.where(mine, jnp.sum(valid), 0.0), jnp.where(mine...]
    unnamed x14 -> x11, local copies, waits for them, and re-layouts: 25.4 us -> 5.48 us
    reduce_sum x15 -> x3, other arithmetic: 19.7 us -> 1.84 us  [the longest x1 0.64 us: shards(): jnp.sum(valid)]
    all_to_all x1 -> x0, local copies, waits for them, and re-layouts: 10.1 us -> none  [shards(): lax.all_to_all(cotangent, 'seq', split_axis=1, concat_axis=2, tiled=True)[0]]
    dynamic_slice x14 -> x0, local copies, waits for them, and re-layouts: 8.21 us -> none  [head_step(): slope = lax.dynamic_index_in_dim(slopes, head, keepdims=False)]
  transfers between devices with their start and end apart: 5 -> 5, of which waited for: 2 -> 2; matrix products, arithmetic and copies ran while one was open for 1% -> 2% of each run, Pallas kernels for 0% -> 13%
where the time goes in v1:
time: 165 us
  blocking collectives  65.5 us (40%)
  Pallas kernels  52.3 us (32%)
  waiting for transfers between devices  17.5 us (11%)
  starting transfers between devices  16.6 us (10%)
  local copies, waits for them, and re-layouts  5.55 us (3%)
  other arithmetic  3.85 us (2%)
  between operations  3.44 us (2%)
    psum x1, blocking collectives, shards(): lax.psum(jnp.stack([jnp.where(mine, jnp.sum(valid), 0.0), jnp.where(mine...  65.5 us
    pallas_call x1, Pallas kernels, shards(): pl.pallas_call(functools.partial(grad_kernel, group, key_tiles), grid=(kv...  25.1 us
    pallas_call x1, Pallas kernels, shards(): pl.pallas_call(functools.partial(prob_kernel, group, key_tiles), grid=(kv...  18 us
    ppermute x4, waiting for transfers between devices, passed_along(): lax.ppermute(value, axis, [(source, source + steps) for source in range(l...  17.5 us
    ppermute x4, starting transfers between devices, passed_along(): lax.ppermute(value, axis, [(source, source + steps) for source in range(l...  10.1 us
    pallas_call x2, Pallas kernels, flip_blocks(): pl.pallas_call(flip_kernel, grid=(count,), in_specs=[pl.BlockSpec((rows,...  9.28 us
    all_to_all x1, starting transfers between devices, shards(): lax.all_to_all(flipped, 'seq', split_axis=0, concat_axis=0, tiled=True)  6.52 us
    unnamed x11, local copies, waits for them, and re-layouts  5.48 us
  transfers between devices with their start and end apart: 5, of which 2 were waited for; matrix products, arithmetic and copies ran while one was open for 2% of the time, Pallas kernels for 13%

profile of v1, /device:TPU:1, one launch (start us, length us, event | category | flops | bytes accessed | tf_op | source)
XLA Modules:
  0.0 164.8 jit_solution(76349323323969556)
XLA Ops:
  0.6 4.0 %copy.11 = bf16[1,4096,224]{2,1,0:T(8,128)(2,1)} copy(bf16[1,4096,224]{1,2,0:T(8,128)(2,1)} %param.11) | data formatting | bytes 3670016 | tf_op args[3]
  4.6 6.0 %flip_blocks.2 = bf16[8,224,512]{2,1,0:T(8,128)(2,1)} custom-call(bf16[4096,224]{1,0:T(8,128)(2,1)} %bitcast.22), custom_call_target="tpu_custom_call" | custom-call | tf_op jit(solution)/shard_map/flip_blocks/pallas_call | solution.py:31
  10.6 6.5 %all-to-all-start = ((bf16[8,224,512]{2,1,0:T(8,128)(2,1)}), bf16[8,224,512]{2,1,0:T(8,128)(2,1)S(1)}, u32[]{:S(2)}, u32[]{:S(2)}) async-start(bf16[8,224,512]{2,1,0:T(8,128)(2,1)} %flip_blocks.2), calls=%async_computation | async-start | bytes 3670016 | tf_op jit(solution)/shard_map/all_to_all | solution.py:156
  17.2 3.5 %collective-permute-start.1 = (bf16[512,512]{1,0:T(8,128)(2,1)S(1)}, bf16[512,512]{1,0:T(8,128)(2,1)S(1)}, u32[]{:S(2)}, u32[]{:S(2)}) collective-permute-start(bf16[512,512]{1,0:T(8,128)(2,1)S(1)} %pad_maximum_fusion.k_refs_2_.v_refs_2_), channel_id=1, source_target_pairs={{0,1},{1,2},{2,3},{3,4},{4,5},{5,6},{6,7},{8,9},{9,10},{10,11},{11... | collective-permute-start | bytes 1572872 | tf_op jit(solution)/shard_map/ppermute | solution.py:21
  20.7 3.1 %collective-permute-start = (bf16[512,512]{1,0:T(8,128)(2,1)S(1)}, bf16[512,512]{1,0:T(8,128)(2,1)S(1)}, u32[]{:S(2)}, u32[]{:S(2)}) collective-permute-start(bf16[512,512]{1,0:T(8,128)(2,1)S(1)} %pad_maximum_fusion.k_refs_2_.v_refs_2_), channel_id=1, source_target_pairs={{0,2},{1,3},{2,4},{3,5},{4,6},{5,7},{8,10},{9,11},{10,12},{11,13},... | collective-permute-start | bytes 1572872 | tf_op jit(solution)/shard_map/ppermute | solution.py:21
  25.2 0.6 convert_reduce_fusion
  25.8 0.6 and_select_fusion
  26.4 65.5 %psum.7 = f32[2,4]{1,0:T(2,128)S(1)} all-reduce(f32[2,4]{1,0:T(2,128)S(1)} %pad_maximum_fusion.3), channel_id=1, replica_groups=mesh['roll'=4,'seq'=8] {'roll','seq'}, use_global_device_ids=true, to_apply=%region_1.2 | all-reduce | flops 8 | bytes 64 | tf_op jit(solution)/shard_map/psum | solution.py:164
  91.9 0.6 slice_reduce_fusion
  93.2 0.0 copy-start.1
  93.2 3.3 %flip_blocks.3 = bf16[1,1792,512]{2,1,0:T(8,128)(2,1)} custom-call(bf16[512,1792]{1,0:T(8,128)(2,1)} %bitcast.23), custom_call_target="tpu_custom_call" | custom-call | tf_op jit(solution)/shard_map/flip_blocks/pallas_call | solution.py:31
  96.5 0.6 fusion.7
  97.8 0.0 collective-permute-done.1.k_refs_1_.v_refs_1_
  97.8 1.5 copy-done
  99.3 18.0 %probs.1 = (bf16[2,4,1152,896]{3,2,1,0:T(8,128)(2,1)}, f32[2,4,144,896]{3,2,1,0:T(8,128)}) custom-call(s32[1]{0:T(128)} %bitcast.10.invalid_ref, f32[14]{0:T(128)S(1)} %copy-done.1, bf16[1792,512]{1,0:T(8,128)(2,1)S(1)} %bitcast.21, bf16[512,512]{1,0:T(8,128)(2,1)S(1)} %collective-permute-done.k_refs_0_.v_refs_0_, ...), custom_call_target="tpu_custom_call" | custom-call | flops 4227858432 | bytes 16515072 | tf_op jit(solution)/shard_map/probs/pallas_call | solution.py:181
  117.3 0.0 all-to-all-done
  117.3 25.1 %grads.1 = (bf16[512,1792]{1,0:T(8,128)(2,1)}, bf16[1024,256]{1,0:T(8,128)(2,1)S(1)}, bf16[1024,256]{1,0:T(8,128)(2,1)S(1)}, f32[512,256]{1,0:T(8,128)S(1)}, f32[512,256]{1,0:T(8,128)S(1)}) custom-call(f32[1]{0:T(128)} %bitcast.3.scale_ref, f32[1,512]{1,0:T(1,128)S(1)} %get-tuple-element.23.keep_ref, bf16[1792,512]{1,0:T(8,128)(2,1)S(1)} %bitcast.19, ...), custom_call_target="tpu_custom_call" | custom-call | flops 8455716864 | bytes 16515072 | tf_op jit(solution)/shard_map/grads/pallas_call | solution.py:205
  142.5 1.3 collective-permute-start.3
  143.9 2.2 %collective-permute-start.2 = (bf16[512,512]{1,0:T(8,128)(2,1)S(1)}, bf16[512,512]{1,0:T(8,128)(2,1)S(1)}, u32[]{:S(2)}, u32[]{:S(2)}) collective-permute-start(bf16[512,512]{1,0:T(8,128)(2,1)S(1)} %pad_maximum_fusion.1), channel_id=1, source_target_pairs={{1,0},{2,1},{3,2},{4,3},{5,4},{6,5},{7,6},{9,8},{10,9},{11,10},{12... | collective-permute-start | bytes 1572872 | tf_op jit(solution)/shard_map/ppermute | solution.py:21
  146.0 11.7 %collective-permute-done.3 = bf16[512,512]{1,0:T(8,128)(2,1)S(1)} collective-permute-done((bf16[512,512]{1,0:T(8,128)(2,1)S(1)}, bf16[512,512]{1,0:T(8,128)(2,1)S(1)}, u32[]{:S(2)}, u32[]{:S(2)}) %collective-permute-start.3) | collective-permute-done | bytes 524320 | tf_op jit(solution)/shard_map/ppermute | solution.py:21
  157.7 0.1 convert_element_type.29
  157.8 5.9 %collective-permute-done.2 = bf16[512,512]{1,0:T(8,128)(2,1)S(1)} collective-permute-done((bf16[512,512]{1,0:T(8,128)(2,1)S(1)}, bf16[512,512]{1,0:T(8,128)(2,1)S(1)}, u32[]{:S(2)}, u32[]{:S(2)}) %collective-permute-start.2) | collective-permute-done | bytes 524320 | tf_op jit(solution)/shard_map/ppermute | solution.py:21
  163.7 0.1 convert_element_type.28
  163.8 1.0 fusion.5
  (16 shorter events, 0.2 us)
Async XLA Ops:
  10.6 6.5 %copy-start.2 = (bf16[1,512,256]{2,1,0:T(8,128)(2,1)S(1)}, bf16[1,512,256]{2,1,0:T(8,128)(2,1)}, u32[]{:S(2)}) copy-start(bf16[1,512,256]{2,1,0:T(8,128)(2,1)} %param.10) | copy-start | bytes 786436
  10.6 6.5 %copy-start.3 = (bf16[1,512,256]{2,1,0:T(8,128)(2,1)S(1)}, bf16[1,512,256]{2,1,0:T(8,128)(2,1)}, u32[]{:S(2)}) copy-start(bf16[1,512,256]{2,1,0:T(8,128)(2,1)} %param.9) | copy-start | bytes 786436
  10.6 14.6 %copy-start.4 = (s32[1,512]{1,0:T(1,128)S(1)}, s32[1,512]{1,0:T(1,128)}, u32[]{:S(2)}) copy-start(s32[1,512]{1,0:T(1,128)} %param.14) | copy-start | bytes 6148
  10.6 106.7 %all-to-all-start = ((bf16[8,224,512]{2,1,0:T(8,128)(2,1)}), bf16[8,224,512]{2,1,0:T(8,128)(2,1)S(1)}, u32[]{:S(2)}, u32[]{:S(2)}) async-start(bf16[8,224,512]{2,1,0:T(8,128)(2,1)} %flip_blocks.2), calls=%async_computation | async-start | bytes 3670016 | tf_op jit(solution)/shard_map/all_to_all | solution.py:156
  17.2 80.6 %collective-permute-start.1 = (bf16[512,512]{1,0:T(8,128)(2,1)S(1)}, bf16[512,512]{1,0:T(8,128)(2,1)S(1)}, u32[]{:S(2)}, u32[]{:S(2)}) collective-permute-start(bf16[512,512]{1,0:T(8,128)(2,1)S(1)} %pad_maximum_fusion.k_refs_2_.v_refs_2_), channel_id=1, source_target_pairs={{0,1},{1,2},{2,3},{3,4},{4,5},{5,6},{6,7},{8,9},{9,10},{10,11},{11... | collective-permute-start | bytes 1572872 | tf_op jit(solution)/shard_map/ppermute | solution.py:21
  20.7 77.1 %collective-permute-start = (bf16[512,512]{1,0:T(8,128)(2,1)S(1)}, bf16[512,512]{1,0:T(8,128)(2,1)S(1)}, u32[]{:S(2)}, u32[]{:S(2)}) collective-permute-start(bf16[512,512]{1,0:T(8,128)(2,1)S(1)} %pad_maximum_fusion.k_refs_2_.v_refs_2_), channel_id=1, source_target_pairs={{0,2},{1,3},{2,4},{3,5},{4,6},{5,7},{8,10},{9,11},{10,12},{11,13},... | collective-permute-start | bytes 1572872 | tf_op jit(solution)/shard_map/ppermute | solution.py:21
  93.2 4.6 %copy-start.1 = (f32[14]{0:T(128)S(1)}, f32[14]{0:T(128)}, u32[]{:S(2)}) copy-start(f32[14]{0:T(128)} %slope_ref.1) | copy-start | bytes 172
  97.8 1.5 copy-start
  142.5 15.2 %collective-permute-start.3 = (bf16[512,512]{1,0:T(8,128)(2,1)S(1)}, bf16[512,512]{1,0:T(8,128)(2,1)S(1)}, u32[]{:S(2)}, u32[]{:S(2)}) collective-permute-start(bf16[512,512]{1,0:T(8,128)(2,1)S(1)} %pad_maximum_fusion.2), channel_id=1, source_target_pairs={{2,0},{3,1},{4,2},{5,3},{6,4},{7,5},{10,8},{11,9},{12,10},{13,11},... | collective-permute-start | bytes 1572872 | tf_op jit(solution)/shard_map/ppermute | solution.py:21
  143.9 19.8 %collective-permute-start.2 = (bf16[512,512]{1,0:T(8,128)(2,1)S(1)}, bf16[512,512]{1,0:T(8,128)(2,1)S(1)}, u32[]{:S(2)}, u32[]{:S(2)}) collective-permute-start(bf16[512,512]{1,0:T(8,128)(2,1)S(1)} %pad_maximum_fusion.1), channel_id=1, source_target_pairs={{1,0},{2,1},{3,2},{4,3},{5,4},{6,5},{7,6},{9,8},{10,9},{11,10},{12... | collective-permute-start | bytes 1572872 | tf_op jit(solution)/shard_map/ppermute | solution.py:21

commit v2 on v1

v2 whole, which is shorter than its diff:
```python
import functools
import math

import jax
import jax.numpy as jnp
from jax import lax
from jax.experimental import pallas as pl
from jax.experimental.pallas import tpu as pltpu
from jax.sharding import PartitionSpec as P

HEAD_DIM = 128
WINDOW = 1024
TILE = 128
FAR = -1e30
LOG2E = math.log2(math.e)
VMEM_LIMIT = 60 << 20
NOTE_ROWS = 16
COVER = 1
COUNT_BASE = 128.0


def passed_along(value, axis, steps):
    count = lax.axis_size(axis)
    leading, last = (max(0, -steps), min(count, count - steps))
    return lax.ppermute(value, axis, [(source, source + steps) for source in range(leading, last)])


def head_of(place, half, near):
    return place // half if near else 1 - place // half


def by_head(value):
    return jnp.concatenate([value[:, n:n + HEAD_DIM] for n in range(0, value.shape[1], HEAD_DIM)], 0)


def flipped_heads(value):
    wide = value.astype(jnp.float32)
    if value.shape[1] == HEAD_DIM:
        return jnp.concatenate([wide[n:n + TILE].T for n in range(0, value.shape[0], TILE)], 1).astype(jnp.bfloat16)
    return jnp.concatenate([wide[:, n:n + TILE].T for n in range(0, value.shape[1], TILE)], 0).astype(jnp.bfloat16)


def gathered(refs, place):
    return [jnp.where(place % 2 == 0, refs[0][...], refs[1][...])] + [ref[...] for ref in refs[2:]]


def split_kernel(half, seq_len, place_ref, length_ref, distance_refs, x_ref, mask_ref, keep_ref, factor_ref, *out_refs):
    place = place_ref[0]
    width, rows = x_ref.shape[0], out_refs[0].shape[1]
    near = place // half
    at = place * rows + lax.broadcasted_iota(jnp.int32, mask_ref.shape, 1)
    keep = jnp.where((at < length_ref[0]) & (mask_ref[...] == 1), 1.0, 0.0)
    keep_ref[...] = keep
    distance = [ref[0].astype(jnp.float32) for ref in distance_refs]
    advantage = (sum(distance) * (1.0 / len(distance)) - distance[0]) * (1.0 / 64.0)
    factor_ref[...] = jnp.full(factor_ref.shape, advantage * seq_len, jnp.float32)
    count = jnp.sum(keep, 1, keepdims=True)
    high = jnp.floor(count * (1.0 / COUNT_BASE))
    notes = jnp.where(lax.broadcasted_iota(jnp.int32, (NOTE_ROWS, rows), 0) == 0, high, count - COUNT_BASE * high)
    for n, out_ref in enumerate(out_refs):
        to = (near if n < half else 1 - near) * half + (place % half + n) % half
        out_ref[:width] = x_ref[:, pl.ds(pl.multiple_of(to * rows, TILE), rows)]
        out_ref[width:] = notes.astype(out_ref.dtype)


def counted(part_refs):
    total = 0.0
    for part_ref in part_refs:
        notes = part_ref[part_ref.shape[0] - NOTE_ROWS:, :128].astype(jnp.float32)
        total = total + COUNT_BASE * notes[:1] + notes[1:2]
    return total


def load_keys(place, k_refs, v_refs, kband, vtband):
    for n, (k, v) in enumerate(zip(gathered(k_refs, place), gathered(v_refs, place))):
        rows = slice(n * k.shape[0], (n + 1) * k.shape[0])
        kband[rows] = k
        vtband[:HEAD_DIM, rows] = v.astype(jnp.float32).T.astype(vtband.dtype)
    vtband[HEAD_DIM:] = jnp.ones(vtband[HEAD_DIM:].shape, vtband.dtype)


def load_grads(place, half, k_refs, v_refs, part_refs, ktband, vband, dk_acc, dv_acc, dt_all):
    for n, (k, v) in enumerate(zip(gathered(k_refs, place), gathered(v_refs, place))):
        rows = slice(n * k.shape[0], (n + 1) * k.shape[0])
        ktband[:, rows] = k.astype(jnp.float32).T.astype(ktband.dtype)
        vband[rows] = v
    dk_acc[...] = jnp.zeros(dk_acc.shape, dk_acc.dtype)
    dv_acc[...] = jnp.zeros(dv_acc.shape, dv_acc.dtype)
    for n, part_ref in enumerate(part_refs):
        width = part_ref.shape[0] - NOTE_ROWS
        source = (place % half + half - n) % half
        part = part_ref[:width].astype(jnp.float32)
        for c in range(dt_all.shape[0]):
            dt_all[c, pl.ds(pl.multiple_of(source * width, 8), width)] = part[:, c * TILE:(c + 1) * TILE]


def slope_lanes(slope_ref, first, group):
    return jnp.concatenate([jnp.full((1, TILE), slope_ref[first + h] * LOG2E, jnp.float32) for h in range(group)], 1)


def load_bias(slope_row, bias):
    bias[...] = lax.broadcasted_iota(jnp.int32, bias.shape, 0).astype(jnp.float32) * slope_row


def soften(sub, place, reach, subs, slope_row, q, kband, vtband, bias, scores, e_ref):
    keys, lanes = scores.shape
    key_tiles = keys // TILE
    scale = LOG2E / math.sqrt(HEAD_DIM)
    qt = flipped_heads(q)
    below = (lax.broadcasted_iota(jnp.int32, (TILE, lanes), 0)
             > lax.broadcasted_iota(jnp.int32, (TILE, lanes), 1) % TILE)
    start = pl.multiple_of(sub * TILE, TILE)
    invalid = jnp.maximum(reach - place, 0) * subs
    peak = None
    shifts = []
    for t in range(key_tiles):
        k_tile = kband[pl.ds(start + t * TILE, TILE)]
        s = jnp.dot(k_tile, qt, preferred_element_type=jnp.float32) * scale + bias[...]
        if t == 0:
            s = jnp.where(below, s, FAR)
        elif t == key_tiles - 1:
            s = jnp.where(below, FAR, s)
        scores[t * TILE:(t + 1) * TILE] = s
        shift = slope_row * (t * TILE) + jnp.where(sub + t < invalid, FAR, 0.0)
        shifts.append(shift)
        top = jnp.max(s.reshape(TILE // 8, 8, lanes), 0) + shift
        peak = top if peak is None else jnp.maximum(peak, top)
    peak = jnp.max(peak, 0, keepdims=True)
    for t in range(key_tiles):
        e = jnp.exp2(scores[t * TILE:(t + 1) * TILE] - (peak - shifts[t]))
        e_ref[t * TILE:(t + 1) * TILE] = e.astype(e_ref.dtype)
    return jnp.dot(vtband[:, pl.ds(start, keys)], e_ref[...], preferred_element_type=jnp.float32)


def differentiate(sub, keep, q, o, e_ref, ktband, vband, dk_acc, dv_acc, ds_all, dt_all):
    keys, lanes = ds_all.shape
    start = pl.multiple_of(sub * TILE, TILE)
    keep = jnp.concatenate([keep] * (lanes // TILE), 1)
    inv = 1.0 / o[HEAD_DIM:HEAD_DIM + 1]
    dt = jnp.concatenate([dt_all[sub, n:n + HEAD_DIM] for n in range(0, lanes, TILE)], 1)
    dt = (dt * (keep * inv)).astype(jnp.bfloat16)
    d = flipped_heads(dt)
    delta = jnp.sum(dt.astype(jnp.float32) * o[:HEAD_DIM], 0, keepdims=True) * inv
    for t in range(keys // TILE):
        rows = pl.ds(start + t * TILE, TILE)
        e = e_ref[t * TILE:(t + 1) * TILE]
        dp = jnp.dot(vband[rows], dt, preferred_element_type=jnp.float32)
        ds = (e.astype(jnp.float32) * (dp - delta)).astype(jnp.bfloat16)
        ds_all[t * TILE:(t + 1) * TILE] = ds
        dv_acc[rows] += jnp.dot(e, d, preferred_element_type=jnp.float32)
        dk_acc[rows] += jnp.dot(ds, q, preferred_element_type=jnp.float32)
    return jnp.dot(ktband[:, pl.ds(start, keys)], ds_all[...], preferred_element_type=jnp.float32)


def store_sums(out_refs, dk_acc, dv_acc):
    for n, out_ref in enumerate(out_refs):
        rows = slice(n * out_ref.shape[0], (n + 1) * out_ref.shape[0])
        out_ref[:, :HEAD_DIM] = dk_acc[rows].astype(out_ref.dtype)
        out_ref[:, HEAD_DIM:] = dv_acc[rows].astype(out_ref.dtype)


def near_kernel(half, reach, place_ref, slope_ref, keep_ref, q_ref, k_refs, v_refs, part_refs,
                dqt_ref, far_two, far_one, own_ref, count_ref,
                kband, vtband, bias, scores, e_all, ktband, vband, dk_acc, dv_acc, ds_all, dt_all):
    place = place_ref[0]
    sub, subs = pl.program_id(0), pl.num_programs(0)
    group = scores.shape[1] // TILE
    slope_row = slope_lanes(slope_ref, head_of(place, half, True) * group, group)

    @pl.when(sub == 0)
    def _():
        load_keys(place, k_refs, v_refs, kband, vtband)
        load_bias(slope_row, bias)
        load_grads(place, half, k_refs, v_refs, part_refs, ktband, vband, dk_acc, dv_acc, dt_all)

    q = by_head(q_ref[...])
    o = soften(sub, place, reach, subs, slope_row, q, kband, vtband, bias, scores, e_all)
    dqt_ref[...] = differentiate(sub, keep_ref[...], q, o, e_all, ktband, vband, dk_acc, dv_acc, ds_all, dt_all)

    @pl.when(sub == subs - 1)
    def _():
        count_ref[...] = jnp.broadcast_to(counted(part_refs), count_ref.shape)
        store_sums((far_two, far_one, own_ref), dk_acc, dv_acc)


def prob_kernel(half, reach, place_ref, slope_ref, q_ref, k_refs, v_refs, e_ref, o_ref, kband, vtband, bias, scores):
    place = place_ref[0]
    sub, subs = pl.program_id(0), pl.num_programs(0)
    group = scores.shape[1] // TILE
    slope_row = slope_lanes(slope_ref, head_of(place, half, False) * group, group)

    @pl.when(sub == 0)
    def _():
        load_keys(place, k_refs, v_refs, kband, vtband)
        load_bias(slope_row, bias)

    o_ref[...] = soften(sub, place, reach, subs, slope_row, by_head(q_ref[...]), kband, vtband, bias, scores, e_ref)


def grad_kernel(half, place_ref, factor_ref, keep_ref, q_ref, k_refs, v_refs, e_ref, o_ref, part_refs, near_dqt, count_ref,
                dq_ref, far_two, far_one, own_ref, weight_ref, ktband, vband, dk_acc, dv_acc, ds_all, dt_all):
    place = place_ref[0]
    sub = pl.program_id(0)
    lanes = ds_all.shape[1]

    @pl.when(sub == 0)
    def _():
        load_grads(place, half, k_refs, v_refs, part_refs, ktband, vband, dk_acc, dv_acc, dt_all)

    dqt = differentiate(sub, keep_ref[...], by_head(q_ref[...]), o_ref, e_ref, ktband, vband, dk_acc, dv_acc, ds_all,
                        dt_all)
    weight = factor_ref[:1] / (1.0 + count_ref[:1] + counted(part_refs))
    weight_ref[...] = jnp.broadcast_to(weight, weight_ref.shape)
    near = place // half
    for first, value in ((near * lanes, near_dqt[...]), ((1 - near) * lanes, dqt)):
        for n in range(0, lanes, TILE):
            cols = pl.ds(pl.multiple_of(first + n, TILE), TILE)
            dq_ref[:, cols] = (value[:, n:n + TILE].T * (weight * (1.0 / math.sqrt(HEAD_DIM)))).astype(dq_ref.dtype)

    @pl.when(sub == pl.num_programs(0) - 1)
    def _():
        store_sums((far_two, far_one, own_ref), dk_acc, dv_acc)


def returned_sums(place, half, total, back_refs, near):
    for n, back_ref in enumerate(back_refs):
        same = ((place + 1 + n) // half == place // half) == near
        back = back_ref[...].astype(jnp.float32)
        total = [total[0] + jnp.where(same, back, 0.0), total[1] + jnp.where(same, 0.0, back)]
    return total


def early_kernel(half, place_ref, own_near, own_other, back_refs, near_total, other_total):
    near_total[...], other_total[...] = returned_sums(
        place_ref[0], half, [own_near[...], own_other[...]], back_refs, True)


def final_kernel(half, place_ref, weight_ref, near_total, other_total, back_refs, dk_ref, dv_ref):
    place = place_ref[0]
    total = returned_sums(place, half, [near_total[...], other_total[...]], back_refs, False)
    high = place // half == 1
    total = [jnp.where(high, total[1], total[0]), jnp.where(high, total[0], total[1])]
    weight = weight_ref[:1, :HEAD_DIM]
    for n, value in enumerate(total):
        cols = slice(n * HEAD_DIM, (n + 1) * HEAD_DIM)
        dk_ref[:, cols] = (value[:, :HEAD_DIM] * (weight * (1.0 / math.sqrt(HEAD_DIM)))).astype(dk_ref.dtype)
        dv_ref[:, cols] = (value[:, HEAD_DIM:] * weight).astype(dv_ref.dtype)


def shards(query_rows, key_rows, value_rows, cotangent, slopes, lengths, loss_mask, distances):
    own_q = query_rows[0]
    own_k = key_rows[0]
    own_v = value_rows[0]
    tok_rows, features = own_q.shape
    kv_features = own_k.shape[1]
    head_count = features // HEAD_DIM
    kv_count = kv_features // HEAD_DIM
    group = head_count // kv_count
    reach = (WINDOW - 2) // tok_rows + 1
    band_len = (reach + 1) * tok_rows
    subs = tok_rows // TILE
    keys = WINDOW + TILE
    lanes = group * TILE
    o_rows = HEAD_DIM + 16
    n_seq = lax.axis_size("seq")
    n_roll = lax.axis_size("roll")
    seq_len = tok_rows * n_seq
    seq_pos = lax.axis_index("seq")
    half = n_seq // kv_count
    width = features // n_seq
    assert kv_count == 2 and width * half == lanes and reach == 2
    place = seq_pos[None].astype(jnp.int32)

    kv_pair = jnp.concatenate([own_k, own_v], 1)
    back_one = passed_along(kv_pair, "seq", 1)
    back_two_even = lax.ppermute(kv_pair, "seq", [(s, s + 2) for s in range(0, n_seq - 2, 2)])

    smem = pl.BlockSpec(memory_space=pltpu.SMEM)
    vmem = pl.BlockSpec(memory_space=pltpu.VMEM)
    params = pltpu.CompilerParams(vmem_limit_bytes=VMEM_LIMIT)
    apart = [distances]
    for shift in range(1, n_roll):
        apart.append(lax.ppermute(distances, "roll", [(n, (n + shift) % n_roll) for n in range(n_roll)]))
    piece = jax.ShapeDtypeStruct((width + NOTE_ROWS, tok_rows), jnp.bfloat16)
    keep, factor, *pieces = pl.pallas_call(
        functools.partial(split_kernel, half, seq_len),
        in_specs=[smem, smem, [smem] * n_roll, vmem, vmem],
        out_specs=[vmem] * (n_seq + 2),
        out_shape=[jax.ShapeDtypeStruct((1, tok_rows), jnp.float32), jax.ShapeDtypeStruct((8, 128), jnp.float32)]
        + [piece] * n_seq,
        compiler_params=params,
        name="split_cotangent",
    )(place, lengths, apart, cotangent[0].T, loss_mask)
    pieces, back_one, back_two_even = lax.optimization_barrier((pieces, back_one, back_two_even))
    parts = {0: pieces[0]}
    for n in list(range(half, n_seq)) + list(range(1, half)):
        pairs = []
        for source in range(n_seq):
            side = source // half if n < half else 1 - source // half
            pairs.append((source, side * half + (source % half + n) % half))
        parts[n] = lax.ppermute(pieces[n], "seq", pairs)
    parts = [parts[n] for n in range(n_seq)]
    back_two_odd = lax.ppermute(back_one, "seq", [(s, s + 1) for s in range(2, n_seq, 2)])
    bands = [back_two_even, back_two_odd, back_one, kv_pair]

    pair_count = group * tok_rows * keys
    bf16, f32 = jnp.bfloat16, jnp.float32

    def head_specs(near, offset):
        spec = pl.BlockSpec((tok_rows, HEAD_DIM), lambda c, at: (0, offset + head_of(at[0], half, near)))
        return [spec] * len(bands)

    def q_spec(near):
        return pl.BlockSpec((TILE, lanes), lambda c, at: (c, head_of(at[0], half, near)))

    keep_spec = pl.BlockSpec((1, TILE), lambda c, at: (0, c))
    e_spec = pl.BlockSpec((None, keys, lanes), lambda c, at: (c, 0, 0))
    o_spec = pl.BlockSpec((None, o_rows, lanes), lambda c, at: (c, 0, 0))
    prob_scratch = [
        pltpu.VMEM((band_len, HEAD_DIM), bf16),
        pltpu.VMEM((o_rows, band_len), bf16),
        pltpu.VMEM((TILE, lanes), f32),
        pltpu.VMEM((keys, lanes), f32),
    ]
    grad_scratch = [
        pltpu.VMEM((HEAD_DIM, band_len), bf16),
        pltpu.VMEM((band_len, HEAD_DIM), bf16),
        pltpu.VMEM((band_len, HEAD_DIM), f32),
        pltpu.VMEM((band_len, HEAD_DIM), f32),
        pltpu.VMEM((keys, lanes), bf16),
        pltpu.VMEM((subs, lanes, TILE), f32),
    ]
    note = jax.ShapeDtypeStruct((8, 128), f32)
    dqt_spec = pl.BlockSpec((None, HEAD_DIM, lanes), lambda c, at: (c, 0, 0))
    grad_shapes = (
        jax.ShapeDtypeStruct((tok_rows, 2 * HEAD_DIM), bf16),
        jax.ShapeDtypeStruct((tok_rows, 2 * HEAD_DIM), bf16),
        jax.ShapeDtypeStruct((tok_rows, 2 * HEAD_DIM), f32),
    )

    def returned(sums):
        return [passed_along(sums[reach - offset], "seq", -offset) for offset in range(1, reach + 1)]

    e_all, o_all = pl.pallas_call(
        functools.partial(prob_kernel, half, reach),
        grid_spec=pltpu.PrefetchScalarGridSpec(
            num_scalar_prefetch=1,
            grid=(subs,),
            in_specs=[smem, q_spec(False), head_specs(False, 0), head_specs(False, kv_count)],
            out_specs=(e_spec, o_spec),
            scratch_shapes=prob_scratch,
        ),
        out_shape=(jax.ShapeDtypeStruct((subs, keys, lanes), bf16), jax.ShapeDtypeStruct((subs, o_rows, lanes), f32)),
        compiler_params=params,
        cost_estimate=pl.CostEstimate(flops=4 * pair_count * HEAD_DIM // COVER, transcendentals=0, bytes_accessed=1 << 16),
        name="other_probs",
    )(place, slopes, own_q, bands, bands)
    late_slopes, o_all = lax.optimization_barrier((slopes, o_all))
    near_dqt, *near_sums, near_count = pl.pallas_call(
        functools.partial(near_kernel, half, reach),
        grid_spec=pltpu.PrefetchScalarGridSpec(
            num_scalar_prefetch=1,
            grid=(subs,),
            in_specs=[smem, keep_spec, q_spec(True), head_specs(True, 0), head_specs(True, kv_count), [vmem] * half],
            out_specs=(dqt_spec, vmem, vmem, vmem, vmem),
            scratch_shapes=prob_scratch + [pltpu.VMEM((keys, lanes), bf16)] + grad_scratch,
        ),
        out_shape=(jax.ShapeDtypeStruct((subs, HEAD_DIM, lanes), f32),) + grad_shapes + (note,),
        compiler_params=params,
        cost_estimate=pl.CostEstimate(flops=12 * pair_count * HEAD_DIM // COVER, transcendentals=0, bytes_accessed=1 << 16),
        name="near_head",
    )(place, late_slopes, keep, own_q, bands, bands, parts[:half])
    near_back = returned(near_sums)
    dq, *other_sums, weight = pl.pallas_call(
        functools.partial(grad_kernel, half),
        grid_spec=pltpu.PrefetchScalarGridSpec(
            num_scalar_prefetch=1,
            grid=(subs,),
            in_specs=[vmem, keep_spec, q_spec(False), head_specs(False, 0), head_specs(False, kv_count), e_spec, o_spec,
                      [vmem] * half, dqt_spec, vmem],
            out_specs=(pl.BlockSpec((TILE, features), lambda c, at: (c, 0)), vmem, vmem, vmem, vmem),
            scratch_shapes=grad_scratch,
        ),
        out_shape=(jax.ShapeDtypeStruct((tok_rows, features), bf16),) + grad_shapes + (note,),
        compiler_params=params,
        cost_estimate=pl.CostEstimate(flops=8 * pair_count * HEAD_DIM // COVER, transcendentals=0, bytes_accessed=1 << 16),
        name="other_grads",
    )(place, factor, keep, own_q, bands, bands, e_all, o_all, parts[half:], near_dqt, near_count)
    other_back = returned(other_sums)

    sums = jax.ShapeDtypeStruct((tok_rows, 2 * HEAD_DIM), f32)
    totals = pl.pallas_call(
        functools.partial(early_kernel, half),
        in_specs=[smem, vmem, vmem, [vmem] * reach],
        out_specs=(vmem, vmem),
        out_shape=(sums, sums),
        name="sum_near",
    )(place, near_sums[-1], other_sums[-1], near_back)
    out = jax.ShapeDtypeStruct((tok_rows, kv_features), bf16)
    grad_k, grad_v = pl.pallas_call(
        functools.partial(final_kernel, half),
        in_specs=[smem, vmem, vmem, vmem, [vmem] * reach],
        out_specs=(vmem, vmem),
        out_shape=(out, out),
        name="sum_other",
    )(place, weight, *totals, other_back)
    return (dq[None], grad_k[None], grad_v[None])


def solution(mesh):
    placed = (
        P("roll", "seq", None),
        P("roll", "seq", None),
        P("roll", "seq", None),
        P("roll", None, "seq"),
        P(),
        P("roll"),
        P("roll", "seq"),
        P("roll"),
    )
    return jax.shard_map(
        shards,
        mesh=mesh,
        in_specs=placed,
        out_specs=(P("roll", "seq", None), P("roll", "seq", None), P("roll", "seq", None)),
        check_vma=False,
    )
```

time: 165 us -> 102 us (0.62); the launches traced: 165 us -> 100 us
  blocking collectives: 65.5 us -> 0 us
  starting transfers between devices: 16.6 us -> 31.6 us
  waiting for transfers between devices: 17.5 us -> 6.73 us
  Pallas kernels: 52.3 us -> 55.4 us
  other arithmetic: 3.85 us -> 1.07 us
  local copies, waits for them, and re-layouts: 5.55 us -> 3.01 us
    psum x1 -> x0, blocking collectives: 65.5 us -> none  [shards(): lax.psum(jnp.stack([jnp.where(mine, jnp.sum(valid), 0.0), jnp.where(mine...]
    ppermute x0 -> x12, starting transfers between devices: none -> 14.8 us  [the longest x7 9.71 us: shards(): parts[n] = lax.ppermute(pieces[n], 'seq', pairs)]
    ppermute x4 -> x5, waiting for transfers between devices: 17.5 us -> 6.58 us  [passed_along(): lax.ppermute(value, axis, [(source, source + steps) for source in range(l...]
    ppermute x4 -> x5, starting transfers between devices: 10.1 us -> 16.8 us  [passed_along(): lax.ppermute(value, axis, [(source, source + steps) for source in range(l...]
    all_to_all x1 -> x0, starting transfers between devices: 6.52 us -> none  [shards(): lax.all_to_all(flipped, 'seq', split_axis=0, concat_axis=0, tiled=True)]
    pallas_call x4 -> x6, Pallas kernels: 52.3 us -> 55.4 us  [the longest x1 20.6 us: shards(): pl.pallas_call(functools.partial(near_kernel, half, reach), grid_spec=plt...]
    unnamed x11 -> x34, local copies, waits for them, and re-layouts: 5.48 us -> 3.01 us
    reduce_sum x3 -> x0, other arithmetic: 1.84 us -> none  [the longest x1 0.64 us: shards(): jnp.sum(valid)]
  transfers between devices with their start and end apart: 5 -> 17, of which waited for: 2 -> 3; matrix products, arithmetic and copies ran while one was open for 2% -> 0% of each run, Pallas kernels for 13% -> 53%
where the time goes in v2:
time: 102 us; the launch traced here: 100 us
  Pallas kernels  55.4 us (54%)
  starting transfers between devices  31.6 us (31%)
  waiting for transfers between devices  6.73 us (7%)
  local copies, waits for them, and re-layouts  3.01 us (3%)
  between operations  2.27 us (2%)
  other arithmetic  1.07 us (1%)
    pallas_call x1, Pallas kernels, shards(): pl.pallas_call(functools.partial(near_kernel, half, reach), grid_spec=plt...  20.6 us
    ppermute x5, starting transfers between devices, passed_along(): lax.ppermute(value, axis, [(source, source + steps) for source in range(l...  16.8 us
    pallas_call x1, Pallas kernels, shards(): pl.pallas_call(functools.partial(grad_kernel, half), grid_spec=pltpu.Pref...  14 us
    pallas_call x1, Pallas kernels, shards(): pl.pallas_call(functools.partial(prob_kernel, half, reach), grid_spec=plt...  11.2 us
    ppermute x7, starting transfers between devices, shards(): parts[n] = lax.ppermute(pieces[n], 'seq', pairs)  9.71 us
    ppermute x5, waiting for transfers between devices, passed_along(): lax.ppermute(value, axis, [(source, source + steps) for source in range(l...  6.58 us
    pallas_call x1, Pallas kernels, shards(): pl.pallas_call(functools.partial(split_kernel, half, seq_len), in_specs=[...  4.79 us
    ppermute x3, starting transfers between devices, shards(): lax.ppermute(distances, 'roll', [(n, (n + shift) % n_roll) for n in range...  3.67 us
  transfers between devices with their start and end apart: 17, of which 3 were waited for; matrix products, arithmetic and copies ran while one was open for 0% of the time, Pallas kernels for 53%

profile of v2, /device:TPU:1, one launch (start us, length us, event | category | flops | bytes accessed | tf_op | source)
XLA Modules:
  0.0 100.1 jit_solution(1648080230576523961)
XLA Ops:
  0.6 1.1 %pad_maximum_fusion.k_refs_3_.v_refs_3_ = bf16[512,512]{1,0:T(8,128)(2,1)S(1)} fusion(bf16[512,256]{1,0:T(8,128)(2,1)} %bitcast.14, bf16[512,256]{1,0:T(8,128)(2,1)} %bitcast.15), kind=kLoop, calls=%fused_computation | loop fusion | flops 1048576 | bytes 1048576 | tf_op jit(solution)/shard_map/concatenate | solution.py:274
  1.7 0.7 collective-permute-start.4
  2.4 7.4 %collective-permute-start.3 = (bf16[512,512]{1,0:T(8,128)(2,1)S(1)}, bf16[512,512]{1,0:T(8,128)(2,1)S(1)}, u32[]{:S(2)}, u32[]{:S(2)}) collective-permute-start(bf16[512,512]{1,0:T(8,128)(2,1)S(1)} %pad_maximum_fusion.k_refs_3_.v_refs_3_), channel_id=1, source_target_pairs={{0,1},{1,2},{2,3},{3,4},{4,5},{5,6},{6,7},{8,9},{9,10},{10,11},{11... | collective-permute-start | bytes 1572872 | tf_op jit(solution)/shard_map/ppermute | solution.py:25
  9.8 1.3 %collective-permute-start.1 = (s32[1]{0:T(128)}, s32[1]{0:T(128)}, u32[]{:S(2)}, u32[]{:S(2)}) collective-permute-start(s32[1]{0:T(128)} %param.15), channel_id=1, source_target_pairs={{0,16},{8,24},{16,0},{24,8},{1,17},{9,25},{17,1},{25,9},{2,18},{10... | collective-permute-start | bytes 20 | tf_op jit(solution)/shard_map/ppermute | solution.py:283
  11.1 1.2 %collective-permute-start = (s32[1]{0:T(128)}, s32[1]{0:T(128)}, u32[]{:S(2)}, u32[]{:S(2)}) collective-permute-start(s32[1]{0:T(128)} %param.15), channel_id=1, source_target_pairs={{0,8},{8,16},{16,24},{24,0},{1,9},{9,17},{17,25},{25,1},{2,10},{10... | collective-permute-start | bytes 20 | tf_op jit(solution)/shard_map/ppermute | solution.py:283
  12.3 1.2 %collective-permute-start.2 = (s32[1]{0:T(128)}, s32[1]{0:T(128)}, u32[]{:S(2)}, u32[]{:S(2)}) collective-permute-start(s32[1]{0:T(128)} %param.15), channel_id=1, source_target_pairs={{0,24},{8,0},{16,8},{24,16},{1,25},{9,1},{17,9},{25,17},{2,26},{10... | collective-permute-start | bytes 20 | tf_op jit(solution)/shard_map/ppermute | solution.py:283
  15.0 4.8 %split_cotangent.1 = (f32[1,512]{1,0:T(1,128)}, f32[8,128]{1,0:T(8,128)}, bf16[240,512]{1,0:T(8,128)(2,1)}, bf16[240,512]{1,0:T(8,128)(2,1)}, bf16[240,512]{1,0:...) custom-call(s32[1]{0:T(128)} %bitcast.place_ref, ...), custom_call_target="tpu_custom_call" | custom-call | tf_op jit(solution)/shard_map/split_cotangent/pallas_call | solution.py:285
  19.8 0.7 collective-permute-start.5
  20.5 3.2 %collective-permute-start.10 = (bf16[240,512]{1,0:T(8,128)(2,1)}, bf16[240,512]{1,0:T(8,128)(2,1)S(1)}, u32[]{:S(2)}, u32[]{:S(2)}) collective-permute-start(bf16[240,512]{1,0:T(8,128)(2,1)} %get-tuple-element.62), channel_id=1, source_target_pairs={{0,1},{1,2},{2,3},{3,0},{4,5},{5,6},{6,7},{7,4},{8,9},{9,10},{10,1... | collective-permute-start | bytes 737288 | tf_op jit(solution)/shard_map/ppermute | solution.py:301
  24.1 1.1 %collective-permute-start.6 = (bf16[240,512]{1,0:T(8,128)(2,1)}, bf16[240,512]{1,0:T(8,128)(2,1)S(1)}, u32[]{:S(2)}, u32[]{:S(2)}) collective-permute-start(bf16[240,512]{1,0:T(8,128)(2,1)} %get-tuple-element.56), channel_id=1, source_target_pairs={{0,4},{1,5},{2,6},{3,7},{4,0},{5,1},{6,2},{7,3},{8,12},{9,13},{10,... | collective-permute-start | bytes 737288 | tf_op jit(solution)/shard_map/ppermute | solution.py:301
  25.3 2.5 %collective-permute-start.7 = (bf16[240,512]{1,0:T(8,128)(2,1)}, bf16[240,512]{1,0:T(8,128)(2,1)S(1)}, u32[]{:S(2)}, u32[]{:S(2)}) collective-permute-start(bf16[240,512]{1,0:T(8,128)(2,1)} %get-tuple-element.57), channel_id=1, source_target_pairs={{0,5},{1,6},{2,7},{3,4},{4,1},{5,2},{6,3},{7,0},{8,13},{9,14},{10,... | collective-permute-start | bytes 737288 | tf_op jit(solution)/shard_map/ppermute | solution.py:301
  27.8 11.2 %other_probs.1 = (bf16[4,1152,896]{2,1,0:T(8,128)(2,1)}, f32[4,144,896]{2,1,0:T(8,128)}) custom-call(s32[1]{0:T(128)} %bitcast.place_ref, f32[14]{0:T(128)} %slope_ref.2, bf16[512,1792]{1,0:T(8,128)(2,1)} %bitcast.11, bf16[512,512]{1,0:T(8,128)(2,1)} %copy-done.1, bf16[512,512]{1,0:T(8,128)(2,1)} %copy-done.3, bf16[512,512]{1,0:T(8,128)(2,1)} %copy-done.2, ...), custom_call_target="tpu_custom_call" | custom-call | flops 2113929216 | bytes 65536 | tf_op jit(solution)/shard_map/other_probs/pallas_call | solution.py:344
  39.1 2.3 %collective-permute-start.8 = (bf16[240,512]{1,0:T(8,128)(2,1)S(1)}, bf16[240,512]{1,0:T(8,128)(2,1)S(1)}, u32[]{:S(2)}, u32[]{:S(2)}) collective-permute-start(bf16[240,512]{1,0:T(8,128)(2,1)S(1)} %copy-done.13), channel_id=1, source_target_pairs={{0,6},{1,7},{2,4},{3,5},{4,2},{5,3},{6,0},{7,1},{8,14},{9,15},{10,... | collective-permute-start | bytes 737288 | tf_op jit(solution)/shard_map/ppermute | solution.py:301
  42.2 20.6 %near_head.1 = (f32[4,128,896]{2,1,0:T(8,128)}, bf16[512,256]{1,0:T(8,128)(2,1)}, bf16[512,256]{1,0:T(8,128)(2,1)}, f32[512,256]{1,0:T(8,128)}, f32[8,128]{1,0:T(8,128)}) custom-call(s32[1]{0:T(128)} %bitcast.place_ref, f32[14]{0:T(128)} %slope_ref.2, f32[1,512]{1,0:T(1,128)} %get-tuple-element.42.keep_ref, bf16[512,1792]{1,0:T(8,128)(2,1)} %bitcast.12, ...), custom_call_target="tpu_custom_call" | custom-call | flops 6341787648 | bytes 65536 | tf_op jit(solution)/shard_map/near_head/pallas_call | solution.py:359
  62.8 4.9 %collective-permute-start.13 = (bf16[512,256]{1,0:T(8,128)(2,1)}, bf16[512,256]{1,0:T(8,128)(2,1)S(1)}, u32[]{:S(2)}, u32[]{:S(2)}) collective-permute-start(bf16[512,256]{1,0:T(8,128)(2,1)} %get-tuple-element.71), channel_id=1, source_target_pairs={{1,0},{2,1},{3,2},{4,3},{5,4},{6,5},{7,6},{9,8},{10,9},{11,10},{12... | collective-permute-start | bytes 786440 | tf_op jit(solution)/shard_map/ppermute | solution.py:25
  67.8 1.3 %collective-permute-start.14 = (bf16[512,256]{1,0:T(8,128)(2,1)}, bf16[512,256]{1,0:T(8,128)(2,1)S(1)}, u32[]{:S(2)}, u32[]{:S(2)}) collective-permute-start(bf16[512,256]{1,0:T(8,128)(2,1)} %get-tuple-element.72), channel_id=1, source_target_pairs={{2,0},{3,1},{4,2},{5,3},{6,4},{7,5},{10,8},{11,9},{12,10},{13,11},... | collective-permute-start | bytes 786440 | tf_op jit(solution)/shard_map/ppermute | solution.py:25
  70.0 14.0 %other_grads.1 = (bf16[512,1792]{1,0:T(8,128)(2,1)}, bf16[512,256]{1,0:T(8,128)(2,1)}, bf16[512,256]{1,0:T(8,128)(2,1)}, f32[512,256]{1,0:T(8,128)}, f32[8,128]{1,0:T(8,128)}) custom-call(s32[1]{0:T(128)} %bitcast.place_ref, f32[8,128]{1,0:T(8,128)} %get-tuple-element.41.factor_ref, f32[1,512]{1,0:T(1,128)} %get-tuple-element.42.keep_ref, ...), custom_call_target="tpu_custom_call" | custom-call | flops 4227858432 | bytes 65536 | tf_op jit(solution)/shard_map/other_grads/pallas_call | solution.py:374
  83.9 1.9 %collective-permute-start.15 = (bf16[512,256]{1,0:T(8,128)(2,1)}, bf16[512,256]{1,0:T(8,128)(2,1)S(1)}, u32[]{:S(2)}, u32[]{:S(2)}) collective-permute-start(bf16[512,256]{1,0:T(8,128)(2,1)} %get-tuple-element.75), channel_id=1, source_target_pairs={{1,0},{2,1},{3,2},{4,3},{5,4},{6,5},{7,6},{9,8},{10,9},{11,10},{12... | collective-permute-start | bytes 786440 | tf_op jit(solution)/shard_map/ppermute | solution.py:25
  85.9 1.3 %collective-permute-start.16 = (bf16[512,256]{1,0:T(8,128)(2,1)}, bf16[512,256]{1,0:T(8,128)(2,1)S(1)}, u32[]{:S(2)}, u32[]{:S(2)}) collective-permute-start(bf16[512,256]{1,0:T(8,128)(2,1)} %get-tuple-element.76), channel_id=1, source_target_pairs={{2,0},{3,1},{4,2},{5,3},{6,4},{7,5},{10,8},{11,9},{12,10},{13,11},... | collective-permute-start | bytes 786440 | tf_op jit(solution)/shard_map/ppermute | solution.py:25
  88.0 2.4 %sum_near.1 = (f32[512,256]{1,0:T(8,128)}, f32[512,256]{1,0:T(8,128)}) custom-call(s32[1]{0:T(128)} %bitcast.place_ref, f32[512,256]{1,0:T(8,128)} %get-tuple-element.69.own_near, f32[512,256]{1,0:T(8,128)} %get-tuple-element.70.own_other, bf16[512,256]{1,0:T(8,128)(2,1)} %copy-done.4, bf16[512,256]{1,0:T(8,128)(2,1)} %copy-done.5), custom_call_target="tpu_custom_call" | custom-call | tf_op jit(solution)/shard_map/sum_near/pallas_call | solution.py:392
  90.4 2.2 %collective-permute-done.15.back_refs_0_ = bf16[512,256]{1,0:T(8,128)(2,1)S(1)} collective-permute-done((bf16[512,256]{1,0:T(8,128)(2,1)}, bf16[512,256]{1,0:T(8,128)(2,1)S(1)}, u32[]{:S(2)}, u32[]{:S(2)}) %collective-permute-start.15) | collective-permute-done | bytes 262176 | tf_op jit(solution)/shard_map/ppermute | solution.py:25
  92.6 4.4 %collective-permute-done.16.back_refs_1_ = bf16[512,256]{1,0:T(8,128)(2,1)S(1)} collective-permute-done((bf16[512,256]{1,0:T(8,128)(2,1)}, bf16[512,256]{1,0:T(8,128)(2,1)S(1)}, u32[]{:S(2)}, u32[]{:S(2)}) %collective-permute-start.16) | collective-permute-done | bytes 262176 | tf_op jit(solution)/shard_map/ppermute | solution.py:25
  97.0 0.7 copy-done.7
  97.7 2.4 %sum_other.1 = (bf16[512,256]{1,0:T(8,128)(2,1)}, bf16[512,256]{1,0:T(8,128)(2,1)}) custom-call(s32[1]{0:T(128)} %bitcast.place_ref, f32[8,128]{1,0:T(8,128)} %get-tuple-element.68.weight_ref, f32[512,256]{1,0:T(8,128)} %get-tuple-element.73.near_total, f32[512,256]{1,0:T(8,128)} %get-tuple-element.74.other_total, bf16[512,256]{1,0:T(8,128)(2,1)} %copy-done.6, ...), custom_call_target="tpu_custom_call" | custom-call | tf_op jit(solution)/shard_map/sum_other/pallas_call | solution.py:400
  (51 shorter events, 3.0 us)
Async XLA Ops:
  1.7 26.1 %copy-start = (bf16[512,512]{1,0:T(8,128)(2,1)}, bf16[512,512]{1,0:T(8,128)(2,1)S(1)}, u32[]{:S(2)}) copy-start(bf16[512,512]{1,0:T(8,128)(2,1)S(1)} %pad_maximum_fusion.k_refs_3_.v_refs_3_) | copy-start | bytes 1572868
  1.7 18.0 %collective-permute-start.4 = (bf16[512,512]{1,0:T(8,128)(2,1)S(1)}, bf16[512,512]{1,0:T(8,128)(2,1)S(1)}, u32[]{:S(2)}, u32[]{:S(2)}) collective-permute-start(bf16[512,512]{1,0:T(8,128)(2,1)S(1)} %pad_maximum_fusion.k_refs_3_.v_refs_3_), channel_id=1, source_target_pairs={{0,2},{2,4},{4,6},{8,10},{10,12},{12,14},{16,18},{18,20},{20,22},{... | collective-permute-start | bytes 1572872 | tf_op jit(solution)/shard_map/ppermute | solution.py:276
  2.4 17.3 %collective-permute-start.3 = (bf16[512,512]{1,0:T(8,128)(2,1)S(1)}, bf16[512,512]{1,0:T(8,128)(2,1)S(1)}, u32[]{:S(2)}, u32[]{:S(2)}) collective-permute-start(bf16[512,512]{1,0:T(8,128)(2,1)S(1)} %pad_maximum_fusion.k_refs_3_.v_refs_3_), channel_id=1, source_target_pairs={{0,1},{1,2},{2,3},{3,4},{4,5},{5,6},{6,7},{8,9},{9,10},{10,11},{11... | collective-permute-start | bytes 1572872 | tf_op jit(solution)/shard_map/ppermute | solution.py:25
  9.8 5.0 %collective-permute-start.1 = (s32[1]{0:T(128)}, s32[1]{0:T(128)}, u32[]{:S(2)}, u32[]{:S(2)}) collective-permute-start(s32[1]{0:T(128)} %param.15), channel_id=1, source_target_pairs={{0,16},{8,24},{16,0},{24,8},{1,17},{9,25},{17,1},{25,9},{2,18},{10... | collective-permute-start | bytes 20 | tf_op jit(solution)/shard_map/ppermute | solution.py:283
  11.1 3.7 %collective-permute-start = (s32[1]{0:T(128)}, s32[1]{0:T(128)}, u32[]{:S(2)}, u32[]{:S(2)}) collective-permute-start(s32[1]{0:T(128)} %param.15), channel_id=1, source_target_pairs={{0,8},{8,16},{16,24},{24,0},{1,9},{9,17},{17,25},{25,1},{2,10},{10... | collective-permute-start | bytes 20 | tf_op jit(solution)/shard_map/ppermute | solution.py:283
  12.3 2.6 %collective-permute-start.2 = (s32[1]{0:T(128)}, s32[1]{0:T(128)}, u32[]{:S(2)}, u32[]{:S(2)}) collective-permute-start(s32[1]{0:T(128)} %param.15), channel_id=1, source_target_pairs={{0,24},{8,0},{16,8},{24,16},{1,25},{9,1},{17,9},{25,17},{2,26},{10... | collective-permute-start | bytes 20 | tf_op jit(solution)/shard_map/ppermute | solution.py:283
  19.8 8.1 %copy-start.1 = (bf16[512,512]{1,0:T(8,128)(2,1)}, bf16[512,512]{1,0:T(8,128)(2,1)S(1)}, u32[]{:S(2)}) copy-start(bf16[512,512]{1,0:T(8,128)(2,1)S(1)} %collective-permute-done.4.k_refs_0_.v_refs_0_) | copy-start | bytes 1572868
  19.8 8.0 %copy-start.2 = (bf16[512,512]{1,0:T(8,128)(2,1)}, bf16[512,512]{1,0:T(8,128)(2,1)S(1)}, u32[]{:S(2)}) copy-start(bf16[512,512]{1,0:T(8,128)(2,1)S(1)} %collective-permute-done.3.k_refs_2_.v_refs_2_) | copy-start | bytes 1572868
  19.8 5.5 %collective-permute-start.5 = (bf16[512,512]{1,0:T(8,128)(2,1)S(1)}, bf16[512,512]{1,0:T(8,128)(2,1)S(1)}, u32[]{:S(2)}, u32[]{:S(2)}) collective-permute-start(bf16[512,512]{1,0:T(8,128)(2,1)S(1)} %collective-permute-done.3.k_refs_2_.v_refs_2_), channel_id=1, source_target_pairs={{2,3},{4,5},{6,7},{10,11},{12,13},{14,15},{18,19},{20,21},{22,23},... | collective-permute-start | bytes 1572872 | tf_op jit(solution)/shard_map/ppermute | solution.py:303
  20.5 18.6 %collective-permute-start.10 = (bf16[240,512]{1,0:T(8,128)(2,1)}, bf16[240,512]{1,0:T(8,128)(2,1)S(1)}, u32[]{:S(2)}, u32[]{:S(2)}) collective-permute-start(bf16[240,512]{1,0:T(8,128)(2,1)} %get-tuple-element.62), channel_id=1, source_target_pairs={{0,1},{1,2},{2,3},{3,0},{4,5},{5,6},{6,7},{7,4},{8,9},{9,10},{10,1... | collective-permute-start | bytes 737288 | tf_op jit(solution)/shard_map/ppermute | solution.py:301
  23.7 17.8 %collective-permute-start.11 = (bf16[240,512]{1,0:T(8,128)(2,1)}, bf16[240,512]{1,0:T(8,128)(2,1)S(1)}, u32[]{:S(2)}, u32[]{:S(2)}) collective-permute-start(bf16[240,512]{1,0:T(8,128)(2,1)} %get-tuple-element.63), channel_id=1, source_target_pairs={{0,2},{1,3},{2,0},{3,1},{4,6},{5,7},{6,4},{7,5},{8,10},{9,11},{10,... | collective-permute-start | bytes 737288 | tf_op jit(solution)/shard_map/ppermute | solution.py:301
  23.7 17.8 %collective-permute-start.12 = (bf16[240,512]{1,0:T(8,128)(2,1)}, bf16[240,512]{1,0:T(8,128)(2,1)S(1)}, u32[]{:S(2)}, u32[]{:S(2)}) collective-permute-start(bf16[240,512]{1,0:T(8,128)(2,1)} %get-tuple-element.64), channel_id=1, source_target_pairs={{0,3},{1,0},{2,1},{3,2},{4,7},{5,4},{6,5},{7,6},{8,11},{9,8},{10,9... | collective-permute-start | bytes 737288 | tf_op jit(solution)/shard_map/ppermute | solution.py:301
  24.1 43.6 %collective-permute-start.6 = (bf16[240,512]{1,0:T(8,128)(2,1)}, bf16[240,512]{1,0:T(8,128)(2,1)S(1)}, u32[]{:S(2)}, u32[]{:S(2)}) collective-permute-start(bf16[240,512]{1,0:T(8,128)(2,1)} %get-tuple-element.56), channel_id=1, source_target_pairs={{0,4},{1,5},{2,6},{3,7},{4,0},{5,1},{6,2},{7,3},{8,12},{9,13},{10,... | collective-permute-start | bytes 737288 | tf_op jit(solution)/shard_map/ppermute | solution.py:301
  25.3 2.6 %copy-start.3 = (bf16[512,512]{1,0:T(8,128)(2,1)}, bf16[512,512]{1,0:T(8,128)(2,1)S(1)}, u32[]{:S(2)}) copy-start(bf16[512,512]{1,0:T(8,128)(2,1)S(1)} %collective-permute-done.5.k_refs_1_.v_refs_1_) | copy-start | bytes 1572868
  25.3 43.8 %collective-permute-start.7 = (bf16[240,512]{1,0:T(8,128)(2,1)}, bf16[240,512]{1,0:T(8,128)(2,1)S(1)}, u32[]{:S(2)}, u32[]{:S(2)}) collective-permute-start(bf16[240,512]{1,0:T(8,128)(2,1)} %get-tuple-element.57), channel_id=1, source_target_pairs={{0,5},{1,6},{2,7},{3,4},{4,1},{5,2},{6,3},{7,0},{8,13},{9,14},{10,... | collective-permute-start | bytes 737288 | tf_op jit(solution)/shard_map/ppermute | solution.py:301
  27.8 11.2 %copy-start.13 = (bf16[240,512]{1,0:T(8,128)(2,1)S(1)}, bf16[240,512]{1,0:T(8,128)(2,1)}, u32[]{:S(2)}) copy-start(bf16[240,512]{1,0:T(8,128)(2,1)} %get-tuple-element.58) | copy-start | bytes 737284
  27.8 13.6 %copy-start.12 = (bf16[240,512]{1,0:T(8,128)(2,1)S(1)}, bf16[240,512]{1,0:T(8,128)(2,1)}, u32[]{:S(2)}) copy-start(bf16[240,512]{1,0:T(8,128)(2,1)} %get-tuple-element.59) | copy-start | bytes 737284
  39.1 30.0 %collective-permute-start.8 = (bf16[240,512]{1,0:T(8,128)(2,1)S(1)}, bf16[240,512]{1,0:T(8,128)(2,1)S(1)}, u32[]{:S(2)}, u32[]{:S(2)}) collective-permute-start(bf16[240,512]{1,0:T(8,128)(2,1)S(1)} %copy-done.13), channel_id=1, source_target_pairs={{0,6},{1,7},{2,4},{3,5},{4,2},{5,3},{6,0},{7,1},{8,14},{9,15},{10,... | collective-permute-start | bytes 737288 | tf_op jit(solution)/shard_map/ppermute | solution.py:301
  41.4 27.7 %collective-permute-start.9 = (bf16[240,512]{1,0:T(8,128)(2,1)S(1)}, bf16[240,512]{1,0:T(8,128)(2,1)S(1)}, u32[]{:S(2)}, u32[]{:S(2)}) collective-permute-start(bf16[240,512]{1,0:T(8,128)(2,1)S(1)} %copy-done.12), channel_id=1, source_target_pairs={{0,7},{1,4},{2,5},{3,6},{4,3},{5,0},{6,1},{7,2},{8,15},{9,12},{10,... | collective-permute-start | bytes 737288 | tf_op jit(solution)/shard_map/ppermute | solution.py:301
  62.8 24.4 %collective-permute-start.13 = (bf16[512,256]{1,0:T(8,128)(2,1)}, bf16[512,256]{1,0:T(8,128)(2,1)S(1)}, u32[]{:S(2)}, u32[]{:S(2)}) collective-permute-start(bf16[512,256]{1,0:T(8,128)(2,1)} %get-tuple-element.71), channel_id=1, source_target_pairs={{1,0},{2,1},{3,2},{4,3},{5,4},{6,5},{7,6},{9,8},{10,9},{11,10},{12... | collective-permute-start | bytes 786440 | tf_op jit(solution)/shard_map/ppermute | solution.py:25
  67.8 19.4 %collective-permute-start.14 = (bf16[512,256]{1,0:T(8,128)(2,1)}, bf16[512,256]{1,0:T(8,128)(2,1)S(1)}, u32[]{:S(2)}, u32[]{:S(2)}) collective-permute-start(bf16[512,256]{1,0:T(8,128)(2,1)} %get-tuple-element.72), channel_id=1, source_target_pairs={{2,0},{3,1},{4,2},{5,3},{6,4},{7,5},{10,8},{11,9},{12,10},{13,11},... | collective-permute-start | bytes 786440 | tf_op jit(solution)/shard_map/ppermute | solution.py:25
  83.9 8.7 %collective-permute-start.15 = (bf16[512,256]{1,0:T(8,128)(2,1)}, bf16[512,256]{1,0:T(8,128)(2,1)S(1)}, u32[]{:S(2)}, u32[]{:S(2)}) collective-permute-start(bf16[512,256]{1,0:T(8,128)(2,1)} %get-tuple-element.75), channel_id=1, source_target_pairs={{1,0},{2,1},{3,2},{4,3},{5,4},{6,5},{7,6},{9,8},{10,9},{11,10},{12... | collective-permute-start | bytes 786440 | tf_op jit(solution)/shard_map/ppermute | solution.py:25
  85.9 11.1 %collective-permute-start.16 = (bf16[512,256]{1,0:T(8,128)(2,1)}, bf16[512,256]{1,0:T(8,128)(2,1)S(1)}, u32[]{:S(2)}, u32[]{:S(2)}) collective-permute-start(bf16[512,256]{1,0:T(8,128)(2,1)} %get-tuple-element.76), channel_id=1, source_target_pairs={{2,0},{3,1},{4,2},{5,3},{6,4},{7,5},{10,8},{11,9},{12,10},{13,11},... | collective-permute-start | bytes 786440 | tf_op jit(solution)/shard_map/ppermute | solution.py:25
  92.6 4.4 %copy-start.6 = (bf16[512,256]{1,0:T(8,128)(2,1)}, bf16[512,256]{1,0:T(8,128)(2,1)S(1)}, u32[]{:S(2)}) copy-start(bf16[512,256]{1,0:T(8,128)(2,1)S(1)} %collective-permute-done.15.back_refs_0_) | copy-start | bytes 786436
  (10 other events, 9.7 us)

commit v3 on v2

--- a/solution.py
+++ b/solution.py
@@ -13,9 +13,10 @@
 TILE = 128
 FAR = -1e30
 LOG2E = math.log2(math.e)
-VMEM_LIMIT = 60 << 20
+VMEM_LIMIT = 24 << 20
 NOTE_ROWS = 16
 COVER = 1
+NEAR_COVER = 1
 COUNT_BASE = 128.0
 
 
@@ -44,16 +45,13 @@
     return [jnp.where(place % 2 == 0, refs[0][...], refs[1][...])] + [ref[...] for ref in refs[2:]]
 
 
-def split_kernel(half, seq_len, place_ref, length_ref, distance_refs, x_ref, mask_ref, keep_ref, factor_ref, *out_refs):
+def split_kernel(half, place_ref, length_ref, x_ref, mask_ref, keep_ref, *out_refs):
     place = place_ref[0]
     width, rows = x_ref.shape[0], out_refs[0].shape[1]
     near = place // half
     at = place * rows + lax.broadcasted_iota(jnp.int32, mask_ref.shape, 1)
     keep = jnp.where((at < length_ref[0]) & (mask_ref[...] == 1), 1.0, 0.0)
     keep_ref[...] = keep
-    distance = [ref[0].astype(jnp.float32) for ref in distance_refs]
-    advantage = (sum(distance) * (1.0 / len(distance)) - distance[0]) * (1.0 / 64.0)
-    factor_ref[...] = jnp.full(factor_ref.shape, advantage * seq_len, jnp.float32)
     count = jnp.sum(keep, 1, keepdims=True)
     high = jnp.floor(count * (1.0 / COUNT_BASE))
     notes = jnp.where(lax.broadcasted_iota(jnp.int32, (NOTE_ROWS, rows), 0) == 0, high, count - COUNT_BASE * high)
@@ -278,20 +276,22 @@
     smem = pl.BlockSpec(memory_space=pltpu.SMEM)
     vmem = pl.BlockSpec(memory_space=pltpu.VMEM)
     params = pltpu.CompilerParams(vmem_limit_bytes=VMEM_LIMIT)
+    piece = jax.ShapeDtypeStruct((width + NOTE_ROWS, tok_rows), jnp.bfloat16)
+    keep, *pieces = pl.pallas_call(
+        functools.partial(split_kernel, half),
+        in_specs=[smem, smem, vmem, vmem],
+        out_specs=[vmem] * (n_seq + 1),
+        out_shape=[jax.ShapeDtypeStruct((1, tok_rows), jnp.float32)]
+        + [piece] * n_seq,
+        compiler_params=params,
+        name="split_cotangent",
+    )(place, lengths, cotangent[0].T, loss_mask)
     apart = [distances]
     for shift in range(1, n_roll):
         apart.append(lax.ppermute(distances, "roll", [(n, (n + shift) % n_roll) for n in range(n_roll)]))
-    piece = jax.ShapeDtypeStruct((width + NOTE_ROWS, tok_rows), jnp.bfloat16)
-    keep, factor, *pieces = pl.pallas_call(
-        functools.partial(split_kernel, half, seq_len),
-        in_specs=[smem, smem, [smem] * n_roll, vmem, vmem],
-        out_specs=[vmem] * (n_seq + 2),
-        out_shape=[jax.ShapeDtypeStruct((1, tok_rows), jnp.float32), jax.ShapeDtypeStruct((8, 128), jnp.float32)]
-        + [piece] * n_seq,
-        compiler_params=params,
-        name="split_cotangent",
-    )(place, lengths, apart, cotangent[0].T, loss_mask)
-    pieces, back_one, back_two_even = lax.optimization_barrier((pieces, back_one, back_two_even))
+    pieces, back_one, apart = lax.optimization_barrier((pieces, back_one, apart))
+    apart = [distance[0].astype(jnp.float32) for distance in apart]
+    factor = jnp.broadcast_to((sum(apart) / n_roll - apart[0]) / 64.0 * seq_len, (8, 128))
     parts = {0: pieces[0]}
     for n in list(range(half, n_seq)) + list(range(1, half)):
         pairs = []
@@ -367,7 +367,7 @@
         ),
         out_shape=(jax.ShapeDtypeStruct((subs, HEAD_DIM, lanes), f32),) + grad_shapes + (note,),
         compiler_params=params,
-        cost_estimate=pl.CostEstimate(flops=12 * pair_count * HEAD_DIM // COVER, transcendentals=0, bytes_accessed=1 << 16),
+        cost_estimate=pl.CostEstimate(flops=12 * pair_count * HEAD_DIM // NEAR_COVER, transcendentals=0, bytes_accessed=1 << 16),
         name="near_head",
     )(place, late_slopes, keep, own_q, bands, bands, parts[:half])
     near_back = returned(near_sums)
@@ -394,6 +394,7 @@
         in_specs=[smem, vmem, vmem, [vmem] * reach],
         out_specs=(vmem, vmem),
         out_shape=(sums, sums),
+        compiler_params=pltpu.CompilerParams(vmem_limit_bytes=8 << 20),
         name="sum_near",
     )(place, near_sums[-1], other_sums[-1], near_back)
     out = jax.ShapeDtypeStruct((tok_rows, kv_features), bf16)
@@ -402,6 +403,7 @@
         in_specs=[smem, vmem, vmem, vmem, [vmem] * reach],
         out_specs=(vmem, vmem),
         out_shape=(out, out),
+        compiler_params=pltpu.CompilerParams(vmem_limit_bytes=8 << 20),
         name="sum_other",
     )(place, weight, *totals, other_back)
     return (dq[None], grad_k[None], grad_v[None])

time: 102 us -> 94.4 us (0.925)
  the two profiles are of different devices: /device:TPU:1 before, /device:TPU:8 now
where the time goes in v3:
time: 94.4 us; the launch traced here: 93.9 us
  Pallas kernels  41.7 us (44%)
  starting transfers between devices  28 us (30%)
  waiting for transfers between devices  15.5 us (16%)
  between operations  3.94 us (4%)
  local copies, waits for them, and re-layouts  3.68 us (4%)
  other arithmetic  1.07 us (1%)
    pallas_call x1, Pallas kernels, shards(): pl.pallas_call(functools.partial(near_kernel, half, reach), grid_spec=plt...  19 us
    ppermute x5, starting transfers between devices, passed_along(): lax.ppermute(value, axis, [(source, source + steps) for source in range(l...  12.2 us
    ppermute x5, waiting for transfers between devices, passed_along(): lax.ppermute(value, axis, [(source, source + steps) for source in range(l...  12 us
    pallas_call x1, Pallas kernels, shards(): pl.pallas_call(functools.partial(grad_kernel, half), grid_spec=pltpu.Pref...  11.5 us
    pallas_call x1, Pallas kernels, shards(): pl.pallas_call(functools.partial(prob_kernel, half, reach), grid_spec=plt...  8.89 us
    ppermute x7, starting transfers between devices, shards(): parts[n] = lax.ppermute(pieces[n], 'seq', pairs)  6.59 us
    ppermute x3, starting transfers between devices, shards(): lax.ppermute(distances, 'roll', [(n, (n + shift) % n_roll) for n in range...  4.51 us
    unnamed x10, local copies, waits for them, and re-layouts  3.68 us
  transfers between devices with their start and end apart: 17, of which 4 were waited for; matrix products, arithmetic and copies ran while one was open for 0% of the time, Pallas kernels for 43%

profile of v3, /device:TPU:8, one launch (start us, length us, event | category | flops | bytes accessed | tf_op | source)
XLA Modules:
  0.0 93.9 jit_solution(13591869802446022938)
XLA Ops:
  0.6 1.1 %pad_maximum_fusion.k_refs_3_.v_refs_3_ = bf16[512,512]{1,0:T(8,128)(2,1)S(1)} fusion(bf16[512,256]{1,0:T(8,128)(2,1)} %bitcast.18, bf16[512,256]{1,0:T(8,128)(2,1)} %bitcast.19), kind=kLoop, calls=%fused_computation | loop fusion | flops 1048576 | bytes 1048576 | tf_op jit(solution)/shard_map/concatenate | solution.py:272
  1.7 1.9 %collective-permute-start = (bf16[512,512]{1,0:T(8,128)(2,1)S(1)}, bf16[512,512]{1,0:T(8,128)(2,1)S(1)}, u32[]{:S(2)}, u32[]{:S(2)}) collective-permute-start(bf16[512,512]{1,0:T(8,128)(2,1)S(1)} %pad_maximum_fusion.k_refs_3_.v_refs_3_), channel_id=1, source_target_pairs={{0,1},{1,2},{2,3},{3,4},{4,5},{5,6},{6,7},{8,9},{9,10},{10,11},{11... | collective-permute-start | bytes 1572872 | tf_op jit(solution)/shard_map/ppermute | solution.py:26
  3.6 1.6 %collective-permute-start.2 = (s32[1]{0:T(128)}, s32[1]{0:T(128)}, u32[]{:S(2)}, u32[]{:S(2)}) collective-permute-start(s32[1]{0:T(128)} %param.15), channel_id=1, source_target_pairs={{0,16},{8,24},{16,0},{24,8},{1,17},{9,25},{17,1},{25,9},{2,18},{10... | collective-permute-start | bytes 20 | tf_op jit(solution)/shard_map/ppermute | solution.py:291
  5.2 1.5 %collective-permute-start.1 = (s32[1]{0:T(128)}, s32[1]{0:T(128)}, u32[]{:S(2)}, u32[]{:S(2)}) collective-permute-start(s32[1]{0:T(128)} %param.15), channel_id=1, source_target_pairs={{0,8},{8,16},{16,24},{24,0},{1,9},{9,17},{17,25},{25,1},{2,10},{10... | collective-permute-start | bytes 20 | tf_op jit(solution)/shard_map/ppermute | solution.py:291
  6.7 1.4 %collective-permute-start.3 = (s32[1]{0:T(128)}, s32[1]{0:T(128)}, u32[]{:S(2)}, u32[]{:S(2)}) collective-permute-start(s32[1]{0:T(128)} %param.15), channel_id=1, source_target_pairs={{0,24},{8,0},{16,8},{24,16},{1,25},{9,1},{17,9},{25,17},{2,26},{10... | collective-permute-start | bytes 20 | tf_op jit(solution)/shard_map/ppermute | solution.py:291
  8.2 3.5 %collective-permute-start.4 = (bf16[512,512]{1,0:T(8,128)(2,1)S(1)}, bf16[512,512]{1,0:T(8,128)(2,1)S(1)}, u32[]{:S(2)}, u32[]{:S(2)}) collective-permute-start(bf16[512,512]{1,0:T(8,128)(2,1)S(1)} %pad_maximum_fusion.k_refs_3_.v_refs_3_), channel_id=1, source_target_pairs={{0,2},{2,4},{4,6},{8,10},{10,12},{12,14},{16,18},{18,20},{20,22},{... | collective-permute-start | bytes 1572872 | tf_op jit(solution)/shard_map/ppermute | solution.py:274
  12.3 1.5 %copy-done = bf16[1,4096,224]{1,2,0:T(8,128)(2,1)S(1)} copy-done((bf16[1,4096,224]{1,2,0:T(8,128)(2,1)S(1)}, bf16[1,4096,224]{1,2,0:T(8,128)(2,1)}, u32[]{:S(2)}) %copy-start) | copy-done | bytes 1835032
  15.5 1.3 %collective-permute-start.5 = (bf16[512,512]{1,0:T(8,128)(2,1)S(1)}, bf16[512,512]{1,0:T(8,128)(2,1)S(1)}, u32[]{:S(2)}, u32[]{:S(2)}) collective-permute-start(bf16[512,512]{1,0:T(8,128)(2,1)S(1)} %collective-permute-done.k_refs_2_.v_refs_2_), channel_id=1, source_target_pairs={{2,3},{4,5},{6,7},{10,11},{12,13},{14,15},{18,19},{20,21},{22,23},... | collective-permute-start | bytes 1572872 | tf_op jit(solution)/shard_map/ppermute | solution.py:303
  17.0 1.7 %collective-permute-start.12 = (bf16[240,512]{1,0:T(8,128)(2,1)}, bf16[240,512]{1,0:T(8,128)(2,1)}, u32[]{:S(2)}, u32[]{:S(2)}) collective-permute-start(bf16[240,512]{1,0:T(8,128)(2,1)} %get-tuple-element.68), channel_id=1, source_target_pairs={{0,3},{1,0},{2,1},{3,2},{4,7},{5,4},{6,5},{7,6},{8,11},{9,8},{10,9... | collective-permute-start | bytes 737288 | tf_op jit(solution)/shard_map/ppermute | solution.py:301
  21.1 2.8 %collective-permute-start.6 = (bf16[240,512]{1,0:T(8,128)(2,1)S(1)}, bf16[240,512]{1,0:T(8,128)(2,1)S(1)}, u32[]{:S(2)}, u32[]{:S(2)}) collective-permute-start(bf16[240,512]{1,0:T(8,128)(2,1)S(1)} %get-tuple-element.60), channel_id=1, source_target_pairs={{0,4},{1,5},{2,6},{3,7},{4,0},{5,1},{6,2},{7,3},{8,12},{9,13},{10,... | collective-permute-start | bytes 737288 | tf_op jit(solution)/shard_map/ppermute | solution.py:301
  23.9 1.5 %copy-done.1 = bf16[1,512,1792]{2,1,0:T(8,128)(2,1)S(1)} copy-done((bf16[1,512,1792]{2,1,0:T(8,128)(2,1)S(1)}, bf16[1,512,1792]{2,1,0:T(8,128)(2,1)}, u32[]{:S(2)}) %copy-start.1) | copy-done | bytes 1835032
  25.4 8.9 %other_probs.1 = (bf16[4,1152,896]{2,1,0:T(8,128)(2,1)S(1)}, f32[4,144,896]{2,1,0:T(8,128)S(1)}) custom-call(s32[1]{0:T(128)} %bitcast.place_ref, f32[14]{0:T(128)S(1)} %copy-done.4, bf16[512,1792]{1,0:T(8,128)(2,1)S(1)} %bitcast.15, bf16[512,512]{1,0:T(8,128)(2,1)S(1)} %collective-permute-done.4.k_refs_0_.v_refs_0_, ...), custom_call_target="tpu_custom_call" | custom-call | flops 2113929216 | bytes 65536 | tf_op jit(solution)/shard_map/other_probs/pallas_call | solution.py:344
  34.3 1.2 %collective-permute-start.8 = (bf16[240,512]{1,0:T(8,128)(2,1)S(1)}, bf16[240,512]{1,0:T(8,128)(2,1)S(1)}, u32[]{:S(2)}, u32[]{:S(2)}) collective-permute-start(bf16[240,512]{1,0:T(8,128)(2,1)S(1)} %get-tuple-element.62), channel_id=1, source_target_pairs={{0,6},{1,7},{2,4},{3,5},{4,2},{5,3},{6,0},{7,1},{8,14},{9,15},{10,... | collective-permute-start | bytes 737288 | tf_op jit(solution)/shard_map/ppermute | solution.py:301
  36.3 19.0 %near_head.1 = (f32[4,128,896]{2,1,0:T(8,128)S(1)}, bf16[512,256]{1,0:T(8,128)(2,1)S(1)}, bf16[512,256]{1,0:T(8,128)(2,1)S(1)}, f32[512,256]{1,0:T(8,128)S(1)}, f32[8,128]{1,0:T(8,128)S(1)}) custom-call(s32[1]{0:T(128)} %bitcast.place_ref, f32[14]{0:T(128)S(1)} %copy-done.4, f32[1,512]{1,0:T(1,128)S(1)} %get-tuple-element.55.keep_ref, ...), custom_call_target="tpu_custom_call" | custom-call | flops 6341787648 | bytes 65536 | tf_op jit(solution)/shard_map/near_head/pallas_call | solution.py:359
  55.4 3.7 %collective-permute-start.13 = (bf16[512,256]{1,0:T(8,128)(2,1)S(1)}, bf16[512,256]{1,0:T(8,128)(2,1)S(1)}, u32[]{:S(2)}, u32[]{:S(2)}) collective-permute-start(bf16[512,256]{1,0:T(8,128)(2,1)S(1)} %get-tuple-element.75), channel_id=1, source_target_pairs={{1,0},{2,1},{3,2},{4,3},{5,4},{6,5},{7,6},{9,8},{10,9},{11,10},{12... | collective-permute-start | bytes 786440 | tf_op jit(solution)/shard_map/ppermute | solution.py:26
  59.0 2.7 %collective-permute-start.14 = (bf16[512,256]{1,0:T(8,128)(2,1)S(1)}, bf16[512,256]{1,0:T(8,128)(2,1)S(1)}, u32[]{:S(2)}, u32[]{:S(2)}) collective-permute-start(bf16[512,256]{1,0:T(8,128)(2,1)S(1)} %get-tuple-element.76), channel_id=1, source_target_pairs={{2,0},{3,1},{4,2},{5,3},{6,4},{7,5},{10,8},{11,9},{12,10},{13,11},... | collective-permute-start | bytes 786440 | tf_op jit(solution)/shard_map/ppermute | solution.py:26
  61.8 1.0 %collective-permute-done.8.part_refs_2_ = bf16[240,512]{1,0:T(8,128)(2,1)S(1)} collective-permute-done((bf16[240,512]{1,0:T(8,128)(2,1)S(1)}, bf16[240,512]{1,0:T(8,128)(2,1)S(1)}, u32[]{:S(2)}, u32[]{:S(2)}) %collective-permute-start.8) | collective-permute-done | bytes 245792 | tf_op jit(solution)/shard_map/ppermute | solution.py:301
  62.8 2.5 %collective-permute-done.9.part_refs_3_ = bf16[240,512]{1,0:T(8,128)(2,1)S(1)} collective-permute-done((bf16[240,512]{1,0:T(8,128)(2,1)S(1)}, bf16[240,512]{1,0:T(8,128)(2,1)S(1)}, u32[]{:S(2)}, u32[]{:S(2)}) %collective-permute-start.9) | collective-permute-done | bytes 245792 | tf_op jit(solution)/shard_map/ppermute | solution.py:301
  65.3 11.5 %other_grads.1 = (bf16[512,1792]{1,0:T(8,128)(2,1)}, bf16[512,256]{1,0:T(8,128)(2,1)S(1)}, bf16[512,256]{1,0:T(8,128)(2,1)S(1)}, f32[512,256]{1,0:T(8,128)S(1)}, f32[8,128]{1,0:T(8,128)S(1)}) custom-call(s32[1]{0:T(128)} %bitcast.place_ref, f32[8,128]{1,0:T(8,128)S(1)} %broadcast_in_dim.16.factor_ref, f32[1,512]{1,0:T(1,128)S(1)} %get-tuple-element.55.keep_ref, ...), custom_call_target="tpu_custom_call" | custom-call | flops 4227858432 | bytes 65536 | tf_op jit(solution)/shard_map/other_grads/pallas_call | solution.py:374
  76.8 1.9 %collective-permute-start.15 = (bf16[512,256]{1,0:T(8,128)(2,1)S(1)}, bf16[512,256]{1,0:T(8,128)(2,1)S(1)}, u32[]{:S(2)}, u32[]{:S(2)}) collective-permute-start(bf16[512,256]{1,0:T(8,128)(2,1)S(1)} %get-tuple-element.79), channel_id=1, source_target_pairs={{1,0},{2,1},{3,2},{4,3},{5,4},{6,5},{7,6},{9,8},{10,9},{11,10},{12... | collective-permute-start | bytes 786440 | tf_op jit(solution)/shard_map/ppermute | solution.py:26
  78.7 1.9 %collective-permute-start.16 = (bf16[512,256]{1,0:T(8,128)(2,1)S(1)}, bf16[512,256]{1,0:T(8,128)(2,1)S(1)}, u32[]{:S(2)}, u32[]{:S(2)}) collective-permute-start(bf16[512,256]{1,0:T(8,128)(2,1)S(1)} %get-tuple-element.80), channel_id=1, source_target_pairs={{2,0},{3,1},{4,2},{5,3},{6,4},{7,5},{10,8},{11,9},{12,10},{13,11},... | collective-permute-start | bytes 786440 | tf_op jit(solution)/shard_map/ppermute | solution.py:26
  80.9 1.7 %collective-permute-done.15.back_refs_0_ = bf16[512,256]{1,0:T(8,128)(2,1)S(1)} collective-permute-done((bf16[512,256]{1,0:T(8,128)(2,1)S(1)}, bf16[512,256]{1,0:T(8,128)(2,1)S(1)}, u32[]{:S(2)}, u32[]{:S(2)}) %collective-permute-start.15) | collective-permute-done | bytes 262176 | tf_op jit(solution)/shard_map/ppermute | solution.py:26
  82.6 10.3 %collective-permute-done.16.back_refs_1_ = bf16[512,256]{1,0:T(8,128)(2,1)S(1)} collective-permute-done((bf16[512,256]{1,0:T(8,128)(2,1)S(1)}, bf16[512,256]{1,0:T(8,128)(2,1)S(1)}, u32[]{:S(2)}, u32[]{:S(2)}) %collective-permute-start.16) | collective-permute-done | bytes 262176 | tf_op jit(solution)/shard_map/ppermute | solution.py:26
  92.9 1.1 %sum_other.1 = (bf16[512,256]{1,0:T(8,128)(2,1)}, bf16[512,256]{1,0:T(8,128)(2,1)}) custom-call(s32[1]{0:T(128)} %bitcast.place_ref, f32[8,128]{1,0:T(8,128)S(1)} %get-tuple-element.72.weight_ref, f32[512,256]{1,0:T(8,128)S(1)} %get-tuple-element.77.near_total, f32[512,256]{1,0:T(8,128)S(1)} %get-tuple-element.78.other_total, ...), custom_call_target="tpu_custom_call" | custom-call | tf_op jit(solution)/shard_map/sum_other/pallas_call | solution.py:401
  (28 shorter events, 2.8 us)
Async XLA Ops:
  0.6 23.3 %copy-start.4 = (f32[14]{0:T(128)S(1)}, f32[14]{0:T(128)}, u32[]{:S(2)}) copy-start(f32[14]{0:T(128)} %slope_ref.2) | copy-start | bytes 172
  1.7 13.8 %collective-permute-start = (bf16[512,512]{1,0:T(8,128)(2,1)S(1)}, bf16[512,512]{1,0:T(8,128)(2,1)S(1)}, u32[]{:S(2)}, u32[]{:S(2)}) collective-permute-start(bf16[512,512]{1,0:T(8,128)(2,1)S(1)} %pad_maximum_fusion.k_refs_3_.v_refs_3_), channel_id=1, source_target_pairs={{0,1},{1,2},{2,3},{3,4},{4,5},{5,6},{6,7},{8,9},{9,10},{10,11},{11... | collective-permute-start | bytes 1572872 | tf_op jit(solution)/shard_map/ppermute | solution.py:26
  3.6 11.8 %collective-permute-start.2 = (s32[1]{0:T(128)}, s32[1]{0:T(128)}, u32[]{:S(2)}, u32[]{:S(2)}) collective-permute-start(s32[1]{0:T(128)} %param.15), channel_id=1, source_target_pairs={{0,16},{8,24},{16,0},{24,8},{1,17},{9,25},{17,1},{25,9},{2,18},{10... | collective-permute-start | bytes 20 | tf_op jit(solution)/shard_map/ppermute | solution.py:291
  5.2 10.2 %collective-permute-start.1 = (s32[1]{0:T(128)}, s32[1]{0:T(128)}, u32[]{:S(2)}, u32[]{:S(2)}) collective-permute-start(s32[1]{0:T(128)} %param.15), channel_id=1, source_target_pairs={{0,8},{8,16},{16,24},{24,0},{1,9},{9,17},{17,25},{25,1},{2,10},{10... | collective-permute-start | bytes 20 | tf_op jit(solution)/shard_map/ppermute | solution.py:291
  6.7 8.7 %collective-permute-start.3 = (s32[1]{0:T(128)}, s32[1]{0:T(128)}, u32[]{:S(2)}, u32[]{:S(2)}) collective-permute-start(s32[1]{0:T(128)} %param.15), channel_id=1, source_target_pairs={{0,24},{8,0},{16,8},{24,16},{1,25},{9,1},{17,9},{25,17},{2,26},{10... | collective-permute-start | bytes 20 | tf_op jit(solution)/shard_map/ppermute | solution.py:291
  8.2 13.0 %collective-permute-start.4 = (bf16[512,512]{1,0:T(8,128)(2,1)S(1)}, bf16[512,512]{1,0:T(8,128)(2,1)S(1)}, u32[]{:S(2)}, u32[]{:S(2)}) collective-permute-start(bf16[512,512]{1,0:T(8,128)(2,1)S(1)} %pad_maximum_fusion.k_refs_3_.v_refs_3_), channel_id=1, source_target_pairs={{0,2},{2,4},{4,6},{8,10},{10,12},{12,14},{16,18},{18,20},{20,22},{... | collective-permute-start | bytes 1572872 | tf_op jit(solution)/shard_map/ppermute | solution.py:274
  12.3 1.5 %copy-start = (bf16[1,4096,224]{1,2,0:T(8,128)(2,1)S(1)}, bf16[1,4096,224]{1,2,0:T(8,128)(2,1)}, u32[]{:S(2)}) copy-start(bf16[1,4096,224]{1,2,0:T(8,128)(2,1)} %param.11) | copy-start | bytes 5505028
  13.8 0.7 copy-start.3
  15.5 8.4 %collective-permute-start.5 = (bf16[512,512]{1,0:T(8,128)(2,1)S(1)}, bf16[512,512]{1,0:T(8,128)(2,1)S(1)}, u32[]{:S(2)}, u32[]{:S(2)}) collective-permute-start(bf16[512,512]{1,0:T(8,128)(2,1)S(1)} %collective-permute-done.k_refs_2_.v_refs_2_), channel_id=1, source_target_pairs={{2,3},{4,5},{6,7},{10,11},{12,13},{14,15},{18,19},{20,21},{22,23},... | collective-permute-start | bytes 1572872 | tf_op jit(solution)/shard_map/ppermute | solution.py:303
  16.8 17.5 %collective-permute-start.10 = (bf16[240,512]{1,0:T(8,128)(2,1)}, bf16[240,512]{1,0:T(8,128)(2,1)}, u32[]{:S(2)}, u32[]{:S(2)}) collective-permute-start(bf16[240,512]{1,0:T(8,128)(2,1)} %get-tuple-element.66), channel_id=1, source_target_pairs={{0,1},{1,2},{2,3},{3,0},{4,5},{5,6},{6,7},{7,4},{8,9},{9,10},{10,1... | collective-permute-start | bytes 737288 | tf_op jit(solution)/shard_map/ppermute | solution.py:301
  16.9 18.7 %collective-permute-start.11 = (bf16[240,512]{1,0:T(8,128)(2,1)}, bf16[240,512]{1,0:T(8,128)(2,1)}, u32[]{:S(2)}, u32[]{:S(2)}) collective-permute-start(bf16[240,512]{1,0:T(8,128)(2,1)} %get-tuple-element.67), channel_id=1, source_target_pairs={{0,2},{1,3},{2,0},{3,1},{4,6},{5,7},{6,4},{7,5},{8,10},{9,11},{10,... | collective-permute-start | bytes 737288 | tf_op jit(solution)/shard_map/ppermute | solution.py:301
  17.0 19.4 %collective-permute-start.12 = (bf16[240,512]{1,0:T(8,128)(2,1)}, bf16[240,512]{1,0:T(8,128)(2,1)}, u32[]{:S(2)}, u32[]{:S(2)}) collective-permute-start(bf16[240,512]{1,0:T(8,128)(2,1)} %get-tuple-element.68), channel_id=1, source_target_pairs={{0,3},{1,0},{2,1},{3,2},{4,7},{5,4},{6,5},{7,6},{8,11},{9,8},{10,9... | collective-permute-start | bytes 737288 | tf_op jit(solution)/shard_map/ppermute | solution.py:301
  21.1 37.9 %collective-permute-start.6 = (bf16[240,512]{1,0:T(8,128)(2,1)S(1)}, bf16[240,512]{1,0:T(8,128)(2,1)S(1)}, u32[]{:S(2)}, u32[]{:S(2)}) collective-permute-start(bf16[240,512]{1,0:T(8,128)(2,1)S(1)} %get-tuple-element.60), channel_id=1, source_target_pairs={{0,4},{1,5},{2,6},{3,7},{4,0},{5,1},{6,2},{7,3},{8,12},{9,13},{10,... | collective-permute-start | bytes 737288 | tf_op jit(solution)/shard_map/ppermute | solution.py:301
  23.9 37.9 %collective-permute-start.7 = (bf16[240,512]{1,0:T(8,128)(2,1)S(1)}, bf16[240,512]{1,0:T(8,128)(2,1)S(1)}, u32[]{:S(2)}, u32[]{:S(2)}) collective-permute-start(bf16[240,512]{1,0:T(8,128)(2,1)S(1)} %get-tuple-element.61), channel_id=1, source_target_pairs={{0,5},{1,6},{2,7},{3,4},{4,1},{5,2},{6,3},{7,0},{8,13},{9,14},{10,... | collective-permute-start | bytes 737288 | tf_op jit(solution)/shard_map/ppermute | solution.py:301
  23.9 1.5 %copy-start.1 = (bf16[1,512,1792]{2,1,0:T(8,128)(2,1)S(1)}, bf16[1,512,1792]{2,1,0:T(8,128)(2,1)}, u32[]{:S(2)}) copy-start(bf16[1,512,1792]{2,1,0:T(8,128)(2,1)} %param.8) | copy-start | bytes 5505028
  25.4 10.9 %copy-start.2 = (bf16[1,512,1792]{2,1,0:T(8,128)(2,1)S(1)}, bf16[1,512,1792]{2,1,0:T(8,128)(2,1)}, u32[]{:S(2)}) copy-start(bf16[1,512,1792]{2,1,0:T(8,128)(2,1)} %param.8) | copy-start | bytes 5505028
  34.3 28.5 %collective-permute-start.8 = (bf16[240,512]{1,0:T(8,128)(2,1)S(1)}, bf16[240,512]{1,0:T(8,128)(2,1)S(1)}, u32[]{:S(2)}, u32[]{:S(2)}) collective-permute-start(bf16[240,512]{1,0:T(8,128)(2,1)S(1)} %get-tuple-element.62), channel_id=1, source_target_pairs={{0,6},{1,7},{2,4},{3,5},{4,2},{5,3},{6,0},{7,1},{8,14},{9,15},{10,... | collective-permute-start | bytes 737288 | tf_op jit(solution)/shard_map/ppermute | solution.py:301
  35.6 29.7 %collective-permute-start.9 = (bf16[240,512]{1,0:T(8,128)(2,1)S(1)}, bf16[240,512]{1,0:T(8,128)(2,1)S(1)}, u32[]{:S(2)}, u32[]{:S(2)}) collective-permute-start(bf16[240,512]{1,0:T(8,128)(2,1)S(1)} %get-tuple-element.63), channel_id=1, source_target_pairs={{0,7},{1,4},{2,5},{3,6},{4,3},{5,0},{6,1},{7,2},{8,15},{9,12},{10,... | collective-permute-start | bytes 737288 | tf_op jit(solution)/shard_map/ppermute | solution.py:301
  55.4 25.3 %collective-permute-start.13 = (bf16[512,256]{1,0:T(8,128)(2,1)S(1)}, bf16[512,256]{1,0:T(8,128)(2,1)S(1)}, u32[]{:S(2)}, u32[]{:S(2)}) collective-permute-start(bf16[512,256]{1,0:T(8,128)(2,1)S(1)} %get-tuple-element.75), channel_id=1, source_target_pairs={{1,0},{2,1},{3,2},{4,3},{5,4},{6,5},{7,6},{9,8},{10,9},{11,10},{12... | collective-permute-start | bytes 786440 | tf_op jit(solution)/shard_map/ppermute | solution.py:26
  59.0 21.6 %collective-permute-start.14 = (bf16[512,256]{1,0:T(8,128)(2,1)S(1)}, bf16[512,256]{1,0:T(8,128)(2,1)S(1)}, u32[]{:S(2)}, u32[]{:S(2)}) collective-permute-start(bf16[512,256]{1,0:T(8,128)(2,1)S(1)} %get-tuple-element.76), channel_id=1, source_target_pairs={{2,0},{3,1},{4,2},{5,3},{6,4},{7,5},{10,8},{11,9},{12,10},{13,11},... | collective-permute-start | bytes 786440 | tf_op jit(solution)/shard_map/ppermute | solution.py:26
  76.8 5.8 %collective-permute-start.15 = (bf16[512,256]{1,0:T(8,128)(2,1)S(1)}, bf16[512,256]{1,0:T(8,128)(2,1)S(1)}, u32[]{:S(2)}, u32[]{:S(2)}) collective-permute-start(bf16[512,256]{1,0:T(8,128)(2,1)S(1)} %get-tuple-element.79), channel_id=1, source_target_pairs={{1,0},{2,1},{3,2},{4,3},{5,4},{6,5},{7,6},{9,8},{10,9},{11,10},{12... | collective-permute-start | bytes 786440 | tf_op jit(solution)/shard_map/ppermute | solution.py:26
  78.7 14.2 %collective-permute-start.16 = (bf16[512,256]{1,0:T(8,128)(2,1)S(1)}, bf16[512,256]{1,0:T(8,128)(2,1)S(1)}, u32[]{:S(2)}, u32[]{:S(2)}) collective-permute-start(bf16[512,256]{1,0:T(8,128)(2,1)S(1)} %get-tuple-element.80), channel_id=1, source_target_pairs={{2,0},{3,1},{4,2},{5,3},{6,4},{7,5},{10,8},{11,9},{12,10},{13,11},... | collective-permute-start | bytes 786440 | tf_op jit(solution)/shard_map/ppermute | solution.py:26

commit v4 on v3

--- a/solution.py
+++ b/solution.py
@@ -14,7 +14,7 @@
 FAR = -1e30
 LOG2E = math.log2(math.e)
 VMEM_LIMIT = 24 << 20
-NOTE_ROWS = 16
+NOTE_ROWS = 8
 COVER = 1
 NEAR_COVER = 1
 COUNT_BASE = 128.0
@@ -195,7 +195,7 @@
     o_ref[...] = soften(sub, place, reach, subs, slope_row, by_head(q_ref[...]), kband, vtband, bias, scores, e_ref)
 
 
-def grad_kernel(half, place_ref, factor_ref, keep_ref, q_ref, k_refs, v_refs, e_ref, o_ref, part_refs, near_dqt, count_ref,
+def grad_kernel(half, seq_len, place_ref, distance_refs, keep_ref, q_ref, k_refs, v_refs, e_ref, o_ref, part_refs, near_dqt, count_ref,
                 dq_ref, far_two, far_one, own_ref, weight_ref, ktband, vband, dk_acc, dv_acc, ds_all, dt_all):
     place = place_ref[0]
     sub = pl.program_id(0)
@@ -207,7 +207,9 @@
 
     dqt = differentiate(sub, keep_ref[...], by_head(q_ref[...]), o_ref, e_ref, ktband, vband, dk_acc, dv_acc, ds_all,
                         dt_all)
-    weight = factor_ref[:1] / (1.0 + count_ref[:1] + counted(part_refs))
+    distance = [ref[:1].astype(jnp.float32) for ref in distance_refs]
+    advantage = (sum(distance) * (1.0 / len(distance)) - distance[0]) * (1.0 / 64.0)
+    weight = advantage * seq_len / (1.0 + count_ref[:1] + counted(part_refs))
     weight_ref[...] = jnp.broadcast_to(weight, weight_ref.shape)
     near = place // half
     for first, value in ((near * lanes, near_dqt[...]), ((1 - near) * lanes, dqt)):
@@ -286,12 +288,11 @@
         compiler_params=params,
         name="split_cotangent",
     )(place, lengths, cotangent[0].T, loss_mask)
-    apart = [distances]
+    spread = jnp.broadcast_to(distances, (8, 128))
+    apart = [spread]
     for shift in range(1, n_roll):
-        apart.append(lax.ppermute(distances, "roll", [(n, (n + shift) % n_roll) for n in range(n_roll)]))
+        apart.append(lax.ppermute(spread, "roll", [(n, (n + shift) % n_roll) for n in range(n_roll)]))
     pieces, back_one, apart = lax.optimization_barrier((pieces, back_one, apart))
-    apart = [distance[0].astype(jnp.float32) for distance in apart]
-    factor = jnp.broadcast_to((sum(apart) / n_roll - apart[0]) / 64.0 * seq_len, (8, 128))
     parts = {0: pieces[0]}
     for n in list(range(half, n_seq)) + list(range(1, half)):
         pairs = []
@@ -372,11 +373,11 @@
     )(place, late_slopes, keep, own_q, bands, bands, parts[:half])
     near_back = returned(near_sums)
     dq, *other_sums, weight = pl.pallas_call(
-        functools.partial(grad_kernel, half),
+        functools.partial(grad_kernel, half, seq_len),
         grid_spec=pltpu.PrefetchScalarGridSpec(
             num_scalar_prefetch=1,
             grid=(subs,),
-            in_specs=[vmem, keep_spec, q_spec(False), head_specs(False, 0), head_specs(False, kv_count), e_spec, o_spec,
+            in_specs=[[vmem] * n_roll, keep_spec, q_spec(False), head_specs(False, 0), head_specs(False, kv_count), e_spec, o_spec,
                       [vmem] * half, dqt_spec, vmem],
             out_specs=(pl.BlockSpec((TILE, features), lambda c, at: (c, 0)), vmem, vmem, vmem, vmem),
             scratch_shapes=grad_scratch,
@@ -385,7 +386,7 @@
         compiler_params=params,
         cost_estimate=pl.CostEstimate(flops=8 * pair_count * HEAD_DIM // COVER, transcendentals=0, bytes_accessed=1 << 16),
         name="other_grads",
-    )(place, factor, keep, own_q, bands, bands, e_all, o_all, parts[half:], near_dqt, near_count)
+    )(place, apart, keep, own_q, bands, bands, e_all, o_all, parts[half:], near_dqt, near_count)
     other_back = returned(other_sums)
 
     sums = jax.ShapeDtypeStruct((tok_rows, 2 * HEAD_DIM), f32)

time: 94.4 us -> 92.3 us (0.978)
  the two profiles are of different devices: /device:TPU:8 before, /device:TPU:1 now
where the time goes in v4:
time: 92.3 us; the launch traced here: 91.7 us
  Pallas kernels  39.8 us (43%)
  starting transfers between devices  38.1 us (41%)
  waiting for transfers between devices  8.35 us (9%)
  local copies, waits for them, and re-layouts  2.19 us (2%)
  between operations  2.14 us (2%)
  other arithmetic  1.07 us (1%)
    pallas_call x1, Pallas kernels, shards(): pl.pallas_call(functools.partial(near_kernel, half, reach), grid_spec=plt...  18.1 us
    ppermute x5, starting transfers between devices, passed_along(): lax.ppermute(value, axis, [(source, source + steps) for source in range(l...  17.5 us
    ppermute x7, starting transfers between devices, shards(): parts[n] = lax.ppermute(pieces[n], 'seq', pairs)  16.3 us
    pallas_call x1, Pallas kernels, shards(): pl.pallas_call(functools.partial(grad_kernel, half, seq_len), grid_spec=p...  11.4 us
    pallas_call x1, Pallas kernels, shards(): pl.pallas_call(functools.partial(prob_kernel, half, reach), grid_spec=plt...  8.87 us
    ppermute x5, waiting for transfers between devices, passed_along(): lax.ppermute(value, axis, [(source, source + steps) for source in range(l...  8.32 us
    ppermute x3, starting transfers between devices, shards(): lax.ppermute(spread, 'roll', [(n, (n + shift) % n_roll) for n in range(n_...  2.76 us
    unnamed x8, local copies, waits for them, and re-layouts  2.18 us
  transfers between devices with their start and end apart: 17, of which 2 were waited for; matrix products, arithmetic and copies ran while one was open for 0% of the time, Pallas kernels for 42%

profile of v4, /device:TPU:1, one launch (start us, length us, event | category | flops | bytes accessed | tf_op | source)
XLA Modules:
  0.0 91.7 jit_solution(10581772940731303093)
XLA Ops:
  0.6 1.1 %pad_maximum_fusion.k_refs_3_.v_refs_3_ = bf16[512,512]{1,0:T(8,128)(2,1)S(1)} fusion(bf16[512,256]{1,0:T(8,128)(2,1)} %bitcast.16, bf16[512,256]{1,0:T(8,128)(2,1)} %bitcast.17), kind=kLoop, calls=%fused_computation | loop fusion | flops 1048576 | bytes 1048576 | tf_op jit(solution)/shard_map/concatenate | solution.py:274
  1.7 4.6 %collective-permute-start = (bf16[512,512]{1,0:T(8,128)(2,1)S(1)}, bf16[512,512]{1,0:T(8,128)(2,1)S(1)}, u32[]{:S(2)}, u32[]{:S(2)}) collective-permute-start(bf16[512,512]{1,0:T(8,128)(2,1)S(1)} %pad_maximum_fusion.k_refs_3_.v_refs_3_), channel_id=1, source_target_pairs={{0,1},{1,2},{2,3},{3,4},{4,5},{5,6},{6,7},{8,9},{9,10},{10,11},{11... | collective-permute-start | bytes 1572872 | tf_op jit(solution)/shard_map/ppermute | solution.py:26
  7.0 2.2 %collective-permute-start.3 = (s32[8,128]{1,0:T(8,128)S(1)}, s32[8,128]{1,0:T(8,128)S(1)}, u32[]{:S(2)}, u32[]{:S(2)}) collective-permute-start(s32[8,128]{1,0:T(8,128)S(1)} %broadcast_in_dim.18.distance_refs_0_), channel_id=1, source_target_pairs={{0,24},{8,0},{16,8},{24,16},{1,25},{9,1},{17,9},{25,17},{2,26},{10... | collective-permute-start | bytes 12296 | tf_op jit(solution)/shard_map/ppermute | solution.py:294
  9.4 0.3 collective-permute-start.1
  9.7 0.7 collective-permute-start.4
  11.1 1.5 %copy-done = bf16[1,4096,224]{1,2,0:T(8,128)(2,1)S(1)} copy-done((bf16[1,4096,224]{1,2,0:T(8,128)(2,1)S(1)}, bf16[1,4096,224]{1,2,0:T(8,128)(2,1)}, u32[]{:S(2)}) %copy-start) | copy-done | bytes 1835032
  12.6 0.7 copy-done.2
  13.5 0.8 collective-permute-start.5
  14.3 4.3 %collective-permute-start.10 = (bf16[232,512]{1,0:T(8,128)(2,1)S(1)}, bf16[232,512]{1,0:T(8,128)(2,1)S(1)}, u32[]{:S(2)}, u32[]{:S(2)}) collective-permute-start(bf16[232,512]{1,0:T(8,128)(2,1)S(1)} %get-tuple-element.66), channel_id=1, source_target_pairs={{0,1},{1,2},{2,3},{3,0},{4,5},{5,6},{6,7},{7,4},{8,9},{9,10},{10,1... | collective-permute-start | bytes 712712 | tf_op jit(solution)/shard_map/ppermute | solution.py:302
  18.6 0.5 collective-permute-start.12
  19.1 2.0 %collective-permute-start.6 = (bf16[232,512]{1,0:T(8,128)(2,1)S(1)}, bf16[232,512]{1,0:T(8,128)(2,1)S(1)}, u32[]{:S(2)}, u32[]{:S(2)}) collective-permute-start(bf16[232,512]{1,0:T(8,128)(2,1)S(1)} %get-tuple-element.60), channel_id=1, source_target_pairs={{0,4},{1,5},{2,6},{3,7},{4,0},{5,1},{6,2},{7,3},{8,12},{9,13},{10,... | collective-permute-start | bytes 712712 | tf_op jit(solution)/shard_map/ppermute | solution.py:302
  21.1 7.3 %collective-permute-start.7 = (bf16[232,512]{1,0:T(8,128)(2,1)S(1)}, bf16[232,512]{1,0:T(8,128)(2,1)S(1)}, u32[]{:S(2)}, u32[]{:S(2)}) collective-permute-start(bf16[232,512]{1,0:T(8,128)(2,1)S(1)} %get-tuple-element.61), channel_id=1, source_target_pairs={{0,5},{1,6},{2,7},{3,4},{4,1},{5,2},{6,3},{7,0},{8,13},{9,14},{10,... | collective-permute-start | bytes 712712 | tf_op jit(solution)/shard_map/ppermute | solution.py:302
  28.4 8.9 %other_probs.1 = (bf16[4,1152,896]{2,1,0:T(8,128)(2,1)S(1)}, f32[4,144,896]{2,1,0:T(8,128)S(1)}) custom-call(s32[1]{0:T(128)} %bitcast.place_ref, f32[14]{0:T(128)S(1)} %copy-done.3, bf16[512,1792]{1,0:T(8,128)(2,1)S(1)} %bitcast.13, bf16[512,512]{1,0:T(8,128)(2,1)S(1)} %collective-permute-done.4.k_refs_0_.v_refs_0_, ...), custom_call_target="tpu_custom_call" | custom-call | flops 2113929216 | bytes 65536 | tf_op jit(solution)/shard_map/other_probs/pallas_call | solution.py:345
  37.3 1.5 %collective-permute-start.8 = (bf16[232,512]{1,0:T(8,128)(2,1)S(1)}, bf16[232,512]{1,0:T(8,128)(2,1)S(1)}, u32[]{:S(2)}, u32[]{:S(2)}) collective-permute-start(bf16[232,512]{1,0:T(8,128)(2,1)S(1)} %get-tuple-element.62), channel_id=1, source_target_pairs={{0,6},{1,7},{2,4},{3,5},{4,2},{5,3},{6,0},{7,1},{8,14},{9,15},{10,... | collective-permute-start | bytes 712712 | tf_op jit(solution)/shard_map/ppermute | solution.py:302
  38.8 0.6 collective-permute-start.9
  39.5 18.1 %near_head.1 = (f32[4,128,896]{2,1,0:T(8,128)S(1)}, bf16[512,256]{1,0:T(8,128)(2,1)S(1)}, bf16[512,256]{1,0:T(8,128)(2,1)S(1)}, f32[512,256]{1,0:T(8,128)S(1)}, f32[8,128]{1,0:T(8,128)S(1)}) custom-call(s32[1]{0:T(128)} %bitcast.place_ref, f32[14]{0:T(128)S(1)} %copy-done.3, f32[1,512]{1,0:T(1,128)S(1)} %get-tuple-element.55.keep_ref, ...), custom_call_target="tpu_custom_call" | custom-call | flops 6341787648 | bytes 65536 | tf_op jit(solution)/shard_map/near_head/pallas_call | solution.py:360
  57.6 3.5 %collective-permute-start.13 = (bf16[512,256]{1,0:T(8,128)(2,1)S(1)}, bf16[512,256]{1,0:T(8,128)(2,1)S(1)}, u32[]{:S(2)}, u32[]{:S(2)}) collective-permute-start(bf16[512,256]{1,0:T(8,128)(2,1)S(1)} %get-tuple-element.75), channel_id=1, source_target_pairs={{1,0},{2,1},{3,2},{4,3},{5,4},{6,5},{7,6},{9,8},{10,9},{11,10},{12... | collective-permute-start | bytes 786440 | tf_op jit(solution)/shard_map/ppermute | solution.py:26
  61.1 1.5 %collective-permute-start.14 = (bf16[512,256]{1,0:T(8,128)(2,1)S(1)}, bf16[512,256]{1,0:T(8,128)(2,1)S(1)}, u32[]{:S(2)}, u32[]{:S(2)}) collective-permute-start(bf16[512,256]{1,0:T(8,128)(2,1)S(1)} %get-tuple-element.76), channel_id=1, source_target_pairs={{2,0},{3,1},{4,2},{5,3},{6,4},{7,5},{10,8},{11,9},{12,10},{13,11},... | collective-permute-start | bytes 786440 | tf_op jit(solution)/shard_map/ppermute | solution.py:26
  62.6 11.4 %other_grads.1 = (bf16[512,1792]{1,0:T(8,128)(2,1)}, bf16[512,256]{1,0:T(8,128)(2,1)S(1)}, bf16[512,256]{1,0:T(8,128)(2,1)S(1)}, f32[512,256]{1,0:T(8,128)S(1)}, f32[8,128]{1,0:T(8,128)S(1)}) custom-call(s32[1]{0:T(128)} %bitcast.place_ref, s32[8,128]{1,0:T(8,128)S(1)} %broadcast_in_dim.18.distance_refs_0_, ...), custom_call_target="tpu_custom_call" | custom-call | flops 4227858432 | bytes 65536 | tf_op jit(solution)/shard_map/other_grads/pallas_call | solution.py:375
  73.9 6.7 %collective-permute-start.15 = (bf16[512,256]{1,0:T(8,128)(2,1)S(1)}, bf16[512,256]{1,0:T(8,128)(2,1)S(1)}, u32[]{:S(2)}, u32[]{:S(2)}) collective-permute-start(bf16[512,256]{1,0:T(8,128)(2,1)S(1)} %get-tuple-element.79), channel_id=1, source_target_pairs={{1,0},{2,1},{3,2},{4,3},{5,4},{6,5},{7,6},{9,8},{10,9},{11,10},{12... | collective-permute-start | bytes 786440 | tf_op jit(solution)/shard_map/ppermute | solution.py:26
  80.7 1.3 %collective-permute-start.16 = (bf16[512,256]{1,0:T(8,128)(2,1)S(1)}, bf16[512,256]{1,0:T(8,128)(2,1)S(1)}, u32[]{:S(2)}, u32[]{:S(2)}) collective-permute-start(bf16[512,256]{1,0:T(8,128)(2,1)S(1)} %get-tuple-element.80), channel_id=1, source_target_pairs={{2,0},{3,1},{4,2},{5,3},{6,4},{7,5},{10,8},{11,9},{12,10},{13,11},... | collective-permute-start | bytes 786440 | tf_op jit(solution)/shard_map/ppermute | solution.py:26
  82.3 0.6 collective-permute-done.15.back_refs_0_
  82.9 7.7 %collective-permute-done.16.back_refs_1_ = bf16[512,256]{1,0:T(8,128)(2,1)S(1)} collective-permute-done((bf16[512,256]{1,0:T(8,128)(2,1)S(1)}, bf16[512,256]{1,0:T(8,128)(2,1)S(1)}, u32[]{:S(2)}, u32[]{:S(2)}) %collective-permute-start.16) | collective-permute-done | bytes 262176 | tf_op jit(solution)/shard_map/ppermute | solution.py:26
  90.6 1.1 %sum_other.1 = (bf16[512,256]{1,0:T(8,128)(2,1)}, bf16[512,256]{1,0:T(8,128)(2,1)}) custom-call(s32[1]{0:T(128)} %bitcast.place_ref, f32[8,128]{1,0:T(8,128)S(1)} %get-tuple-element.72.weight_ref, f32[512,256]{1,0:T(8,128)S(1)} %get-tuple-element.77.near_total, f32[512,256]{1,0:T(8,128)S(1)} %get-tuple-element.78.other_total, ...), custom_call_target="tpu_custom_call" | custom-call | tf_op jit(solution)/shard_map/sum_other/pallas_call | solution.py:402
  (26 shorter events, 0.7 us)
Async XLA Ops:
  0.6 27.8 %copy-start.3 = (f32[14]{0:T(128)S(1)}, f32[14]{0:T(128)}, u32[]{:S(2)}) copy-start(f32[14]{0:T(128)} %slope_ref.2) | copy-start | bytes 172
  1.7 11.7 %collective-permute-start = (bf16[512,512]{1,0:T(8,128)(2,1)S(1)}, bf16[512,512]{1,0:T(8,128)(2,1)S(1)}, u32[]{:S(2)}, u32[]{:S(2)}) collective-permute-start(bf16[512,512]{1,0:T(8,128)(2,1)S(1)} %pad_maximum_fusion.k_refs_3_.v_refs_3_), channel_id=1, source_target_pairs={{0,1},{1,2},{2,3},{3,4},{4,5},{5,6},{6,7},{8,9},{9,10},{10,11},{11... | collective-permute-start | bytes 1572872 | tf_op jit(solution)/shard_map/ppermute | solution.py:26
  7.0 6.4 %collective-permute-start.3 = (s32[8,128]{1,0:T(8,128)S(1)}, s32[8,128]{1,0:T(8,128)S(1)}, u32[]{:S(2)}, u32[]{:S(2)}) collective-permute-start(s32[8,128]{1,0:T(8,128)S(1)} %broadcast_in_dim.18.distance_refs_0_), channel_id=1, source_target_pairs={{0,24},{8,0},{16,8},{24,16},{1,25},{9,1},{17,9},{25,17},{2,26},{10... | collective-permute-start | bytes 12296 | tf_op jit(solution)/shard_map/ppermute | solution.py:294
  9.2 4.2 %collective-permute-start.2 = (s32[8,128]{1,0:T(8,128)S(1)}, s32[8,128]{1,0:T(8,128)S(1)}, u32[]{:S(2)}, u32[]{:S(2)}) collective-permute-start(s32[8,128]{1,0:T(8,128)S(1)} %broadcast_in_dim.18.distance_refs_0_), channel_id=1, source_target_pairs={{0,16},{8,24},{16,0},{24,8},{1,17},{9,25},{17,1},{25,9},{2,18},{10... | collective-permute-start | bytes 12296 | tf_op jit(solution)/shard_map/ppermute | solution.py:294
  9.4 4.0 %collective-permute-start.1 = (s32[8,128]{1,0:T(8,128)S(1)}, s32[8,128]{1,0:T(8,128)S(1)}, u32[]{:S(2)}, u32[]{:S(2)}) collective-permute-start(s32[8,128]{1,0:T(8,128)S(1)} %broadcast_in_dim.18.distance_refs_0_), channel_id=1, source_target_pairs={{0,8},{8,16},{16,24},{24,0},{1,9},{9,17},{17,25},{25,1},{2,10},{10... | collective-permute-start | bytes 12296 | tf_op jit(solution)/shard_map/ppermute | solution.py:294
  9.7 9.4 %collective-permute-start.4 = (bf16[512,512]{1,0:T(8,128)(2,1)S(1)}, bf16[512,512]{1,0:T(8,128)(2,1)S(1)}, u32[]{:S(2)}, u32[]{:S(2)}) collective-permute-start(bf16[512,512]{1,0:T(8,128)(2,1)S(1)} %pad_maximum_fusion.k_refs_3_.v_refs_3_), channel_id=1, source_target_pairs={{0,2},{2,4},{4,6},{8,10},{10,12},{12,14},{16,18},{18,20},{20,22},{... | collective-permute-start | bytes 1572872 | tf_op jit(solution)/shard_map/ppermute | solution.py:276
  11.1 1.5 %copy-start = (bf16[1,4096,224]{1,2,0:T(8,128)(2,1)S(1)}, bf16[1,4096,224]{1,2,0:T(8,128)(2,1)}, u32[]{:S(2)}) copy-start(bf16[1,4096,224]{1,2,0:T(8,128)(2,1)} %param.11) | copy-start | bytes 5505028
  12.6 0.7 copy-start.2
  13.3 15.1 %copy-start.1 = (bf16[1,512,1792]{2,1,0:T(8,128)(2,1)S(1)}, bf16[1,512,1792]{2,1,0:T(8,128)(2,1)}, u32[]{:S(2)}) copy-start(bf16[1,512,1792]{2,1,0:T(8,128)(2,1)} %param.8) | copy-start | bytes 5505028
  13.5 7.6 %collective-permute-start.5 = (bf16[512,512]{1,0:T(8,128)(2,1)S(1)}, bf16[512,512]{1,0:T(8,128)(2,1)S(1)}, u32[]{:S(2)}, u32[]{:S(2)}) collective-permute-start(bf16[512,512]{1,0:T(8,128)(2,1)S(1)} %collective-permute-done.k_refs_2_.v_refs_2_), channel_id=1, source_target_pairs={{2,3},{4,5},{6,7},{10,11},{12,13},{14,15},{18,19},{20,21},{22,23},... | collective-permute-start | bytes 1572872 | tf_op jit(solution)/shard_map/ppermute | solution.py:304
  14.3 23.0 %collective-permute-start.10 = (bf16[232,512]{1,0:T(8,128)(2,1)S(1)}, bf16[232,512]{1,0:T(8,128)(2,1)S(1)}, u32[]{:S(2)}, u32[]{:S(2)}) collective-permute-start(bf16[232,512]{1,0:T(8,128)(2,1)S(1)} %get-tuple-element.66), channel_id=1, source_target_pairs={{0,1},{1,2},{2,3},{3,0},{4,5},{5,6},{6,7},{7,4},{8,9},{9,10},{10,1... | collective-permute-start | bytes 712712 | tf_op jit(solution)/shard_map/ppermute | solution.py:302
  18.6 20.2 %collective-permute-start.11 = (bf16[232,512]{1,0:T(8,128)(2,1)S(1)}, bf16[232,512]{1,0:T(8,128)(2,1)S(1)}, u32[]{:S(2)}, u32[]{:S(2)}) collective-permute-start(bf16[232,512]{1,0:T(8,128)(2,1)S(1)} %get-tuple-element.67), channel_id=1, source_target_pairs={{0,2},{1,3},{2,0},{3,1},{4,6},{5,7},{6,4},{7,5},{8,10},{9,11},{10,... | collective-permute-start | bytes 712712 | tf_op jit(solution)/shard_map/ppermute | solution.py:302
  18.6 20.9 %collective-permute-start.12 = (bf16[232,512]{1,0:T(8,128)(2,1)S(1)}, bf16[232,512]{1,0:T(8,128)(2,1)S(1)}, u32[]{:S(2)}, u32[]{:S(2)}) collective-permute-start(bf16[232,512]{1,0:T(8,128)(2,1)S(1)} %get-tuple-element.68), channel_id=1, source_target_pairs={{0,3},{1,0},{2,1},{3,2},{4,7},{5,4},{6,5},{7,6},{8,11},{9,8},{10,9... | collective-permute-start | bytes 712712 | tf_op jit(solution)/shard_map/ppermute | solution.py:302
  19.1 42.0 %collective-permute-start.6 = (bf16[232,512]{1,0:T(8,128)(2,1)S(1)}, bf16[232,512]{1,0:T(8,128)(2,1)S(1)}, u32[]{:S(2)}, u32[]{:S(2)}) collective-permute-start(bf16[232,512]{1,0:T(8,128)(2,1)S(1)} %get-tuple-element.60), channel_id=1, source_target_pairs={{0,4},{1,5},{2,6},{3,7},{4,0},{5,1},{6,2},{7,3},{8,12},{9,13},{10,... | collective-permute-start | bytes 712712 | tf_op jit(solution)/shard_map/ppermute | solution.py:302
  21.1 41.4 %collective-permute-start.7 = (bf16[232,512]{1,0:T(8,128)(2,1)S(1)}, bf16[232,512]{1,0:T(8,128)(2,1)S(1)}, u32[]{:S(2)}, u32[]{:S(2)}) collective-permute-start(bf16[232,512]{1,0:T(8,128)(2,1)S(1)} %get-tuple-element.61), channel_id=1, source_target_pairs={{0,5},{1,6},{2,7},{3,4},{4,1},{5,2},{6,3},{7,0},{8,13},{9,14},{10,... | collective-permute-start | bytes 712712 | tf_op jit(solution)/shard_map/ppermute | solution.py:302
  37.3 25.3 %collective-permute-start.8 = (bf16[232,512]{1,0:T(8,128)(2,1)S(1)}, bf16[232,512]{1,0:T(8,128)(2,1)S(1)}, u32[]{:S(2)}, u32[]{:S(2)}) collective-permute-start(bf16[232,512]{1,0:T(8,128)(2,1)S(1)} %get-tuple-element.62), channel_id=1, source_target_pairs={{0,6},{1,7},{2,4},{3,5},{4,2},{5,3},{6,0},{7,1},{8,14},{9,15},{10,... | collective-permute-start | bytes 712712 | tf_op jit(solution)/shard_map/ppermute | solution.py:302
  38.8 23.7 %collective-permute-start.9 = (bf16[232,512]{1,0:T(8,128)(2,1)S(1)}, bf16[232,512]{1,0:T(8,128)(2,1)S(1)}, u32[]{:S(2)}, u32[]{:S(2)}) collective-permute-start(bf16[232,512]{1,0:T(8,128)(2,1)S(1)} %get-tuple-element.63), channel_id=1, source_target_pairs={{0,7},{1,4},{2,5},{3,6},{4,3},{5,0},{6,1},{7,2},{8,15},{9,12},{10,... | collective-permute-start | bytes 712712 | tf_op jit(solution)/shard_map/ppermute | solution.py:302
  57.6 24.4 %collective-permute-start.13 = (bf16[512,256]{1,0:T(8,128)(2,1)S(1)}, bf16[512,256]{1,0:T(8,128)(2,1)S(1)}, u32[]{:S(2)}, u32[]{:S(2)}) collective-permute-start(bf16[512,256]{1,0:T(8,128)(2,1)S(1)} %get-tuple-element.75), channel_id=1, source_target_pairs={{1,0},{2,1},{3,2},{4,3},{5,4},{6,5},{7,6},{9,8},{10,9},{11,10},{12... | collective-permute-start | bytes 786440 | tf_op jit(solution)/shard_map/ppermute | solution.py:26
  61.1 20.9 %collective-permute-start.14 = (bf16[512,256]{1,0:T(8,128)(2,1)S(1)}, bf16[512,256]{1,0:T(8,128)(2,1)S(1)}, u32[]{:S(2)}, u32[]{:S(2)}) collective-permute-start(bf16[512,256]{1,0:T(8,128)(2,1)S(1)} %get-tuple-element.76), channel_id=1, source_target_pairs={{2,0},{3,1},{4,2},{5,3},{6,4},{7,5},{10,8},{11,9},{12,10},{13,11},... | collective-permute-start | bytes 786440 | tf_op jit(solution)/shard_map/ppermute | solution.py:26
  73.9 9.0 %collective-permute-start.15 = (bf16[512,256]{1,0:T(8,128)(2,1)S(1)}, bf16[512,256]{1,0:T(8,128)(2,1)S(1)}, u32[]{:S(2)}, u32[]{:S(2)}) collective-permute-start(bf16[512,256]{1,0:T(8,128)(2,1)S(1)} %get-tuple-element.79), channel_id=1, source_target_pairs={{1,0},{2,1},{3,2},{4,3},{5,4},{6,5},{7,6},{9,8},{10,9},{11,10},{12... | collective-permute-start | bytes 786440 | tf_op jit(solution)/shard_map/ppermute | solution.py:26
  80.7 9.9 %collective-permute-start.16 = (bf16[512,256]{1,0:T(8,128)(2,1)S(1)}, bf16[512,256]{1,0:T(8,128)(2,1)S(1)}, u32[]{:S(2)}, u32[]{:S(2)}) collective-permute-start(bf16[512,256]{1,0:T(8,128)(2,1)S(1)} %get-tuple-element.80), channel_id=1, source_target_pairs={{2,0},{3,1},{4,2},{5,3},{6,4},{7,5},{10,8},{11,9},{12,10},{13,11},... | collective-permute-start | bytes 786440 | tf_op jit(solution)/shard_map/ppermute | solution.py:26
